TPU v7x, 512 devices: a whole 4x8x8 slice. The times are simulated.
512 devices in a mesh: gx: 32 (over y, x), gy: 16 (over z, core).
Axes of the slice: x: 4, y: 8, z: 8, core: 2. Of those that a mesh axis runs over, the one named last changes fastest.
Arguments:
- diag_blocks: float32 [9, 2048, 2048], P(None, 'gx', 'gy'), may hold values from 0 to 36, as said below
- edge_blocks: float32 [4, 9, 2048, 2048], P(None, None, 'gx', 'gy'), may hold values from -0.3 to 0.3
- edge_mask: int32 [4, 2048, 2048], P(None, 'gx', 'gy'), may hold values 0 or 1
- src_values: float32 [3, 524288], P(None, ('gx', 'gy')), may hold values from -48 to 48
- src_owner: int32 [524288, 1], P(('gx', 'gy')), may hold values from 0 to 31; in each aligned block of 1024 rows (0 to 1023, 1024 to 2047, ...) at most 64 rows name the same one
- src_node: int32 [524288], P(('gx', 'gy')), may hold values from 0 to 8191
- src_count: int32 [512], P(('gx', 'gy')), may hold values from 256 to 1024, as said below
- surf_node: int32 [1048576], P(('gx', 'gy')), may hold values from 0 to 8191
- surf_param: float32 [3, 1048576], P(None, ('gx', 'gy')), may hold values from 0 to 1
- tile_box: int32 [8192], P(('gx', 'gy')), may hold values from 0 to 511
Outputs:
- adjoint_field: float32 [3, 2048, 2048], P(None, 'gx', 'gy')
- box_gradient: float32 [512, 192], P(('gx', 'gy'))
Inputs may be any that keep to these rules, and one draw needn't show every extreme that they name: `src_owner`: each device's rows name every gx index at most 64 times. `src_count`: some device has all 1024 rows live. `diag_blocks`: entries 0, 4 and 8 lie between 6 and 36; the other entries between 0 and 1.
All inputs are finite; a program needn't handle non-finite values. No bound on the sum of `edge_mask` on one device may be relied on, other than what follows from the above.
Results may differ from a plain program's by a relative error of at most 0.0015.
Values sent between devices are 32-bit elements; how exact they have to be, the bound alone decides.
A program may use at most 64 MiB of HBM per device.

v0:
```python
import jax
import jax.numpy as jnp
from jax import lax
from jax.sharding import PartitionSpec as P

ITERS = 2


def passed_along(block, axis, distance):
    devices = range(lax.axis_size(axis))
    route = [(i - distance, i) for i in devices if i - distance in devices]
    return lax.ppermute(block, axis, route)


def block_product(blocks, field):
    return jnp.stack(
        [
            blocks[row] * field[0] + blocks[3 + row] * field[1] + blocks[6 + row] * field[2]
            for row in range(3)
        ]
    )


def apply_transposed_operator(field, diag_blocks, masked):
    result = block_product(diag_blocks, field)
    toward_upx = block_product(masked[0], field)
    toward_lowx = block_product(masked[1], field)
    toward_upy = block_product(masked[2], field)
    toward_lowy = block_product(masked[3], field)
    from_below_x = passed_along(toward_upx[:, -1:, :], "gx", 1)
    upper_x = jnp.concatenate([from_below_x, toward_upx[:, :-1, :]], axis=1)
    from_above_x = passed_along(toward_lowx[:, :1, :], "gx", -1)
    lower_x = jnp.concatenate([toward_lowx[:, 1:, :], from_above_x], axis=1)
    from_below_y = passed_along(toward_upy[:, :, -1:], "gy", 1)
    upper_y = jnp.concatenate([from_below_y, toward_upy[:, :, :-1]], axis=2)
    from_above_y = passed_along(toward_lowy[:, :, :1], "gy", -1)
    lower_y = jnp.concatenate([toward_lowy[:, :, 1:], from_above_y], axis=2)
    return result + upper_x + lower_x + upper_y + lower_y


def bernstein(coord):
    other = 1.0 - coord
    return jnp.stack(
        [
            other * other * other,
            3.0 * coord * other * other,
            3.0 * coord * coord * other,
            coord * coord * coord,
        ]
    )


def tile_weights(params):
    first = bernstein(params[0])
    second = bernstein(params[1])
    third = bernstein(params[2])
    table = first[:, None, None, :] * second[None, :, None, :] * third[None, None, :, :]
    return table.reshape(64, -1)


def residual_sum(residual, precond):
    return lax.psum(jnp.sum(residual * precond), ("gx", "gy"))


def per_device(
    diag_blocks,
    edge_blocks,
    edge_mask,
    src_values,
    src_owner,
    src_node,
    src_count,
    surf_node,
    surf_param,
    tile_box,
):
    masked = edge_blocks * edge_mask.astype(jnp.float32)[:, None]
    cells_x = diag_blocks.shape[1]
    cells_y = diag_blocks.shape[2]
    rows = src_node.shape[0]
    flat_load = jnp.zeros((3, cells_x * cells_y), jnp.float32)
    all_values, every_owner_index, all_node, all_count = (
        lax.all_gather(src_values, "gx", axis=1, tiled=True),
        lax.all_gather(src_owner, "gx", axis=0, tiled=True),
        lax.all_gather(src_node, "gx", axis=0, tiled=True),
        lax.all_gather(src_count, "gx", axis=0, tiled=True),
    )
    position = jnp.arange(all_node.shape[0], dtype=jnp.int32)
    live = position % rows < jnp.repeat(all_count, rows)
    keeper = live & (every_owner_index[:, 0] == lax.axis_index("gx"))
    flat_load = flat_load.at[:, all_node].add(all_values * keeper.astype(jnp.float32))
    load = flat_load.reshape(3, cells_x, cells_y)
    scale = jnp.stack([diag_blocks[0], diag_blocks[4], diag_blocks[8]])
    solution = jnp.zeros_like(load)
    residual = load
    precond = residual / scale
    search = precond
    norm_now = residual_sum(residual, precond)
    for sweep in range(ITERS):
        image = apply_transposed_operator(search, diag_blocks, masked)
        step_size = norm_now / lax.psum(jnp.sum(search * image), ("gx", "gy"))
        solution = solution + step_size * search
        residual = residual - step_size * image
        if sweep + 1 < ITERS:
            precond = residual / scale
            norm_next = residual_sum(residual, precond)
            search = precond + norm_next / norm_now * search
            norm_now = norm_next
    design_sensitivity = solution.reshape(3, -1)[:, surf_node]
    tile_weight_values = tile_weights(surf_param)
    surface_tiles = tile_box.shape[0]
    series_terms = jnp.einsum(
        "bqe,iqe->qib",
        tile_weight_values.reshape(64, surface_tiles, -1),
        design_sensitivity.reshape(3, surface_tiles, -1),
        precision=lax.Precision.HIGHEST,
    ).reshape(surface_tiles, 192)
    box_count = lax.axis_size("gx") * lax.axis_size("gy")
    onehot = (jnp.arange(box_count, dtype=jnp.int32)[:, None] == tile_box[None, :]).astype(
        jnp.float32
    )
    partial_boxes = jnp.dot(onehot, series_terms, precision=lax.Precision.HIGHEST)
    totals = lax.psum(partial_boxes, ("gx", "gy"))
    gradient = lax.dynamic_slice_in_dim(totals, lax.axis_index(("gx", "gy")), 1, 0)
    return (solution, gradient)


def solution(mesh):
    return jax.shard_map(
        per_device,
        mesh=mesh,
        in_specs=(
            P(None, "gx", "gy"),
            P(None, None, "gx", "gy"),
            P(None, "gx", "gy"),
            P(None, ("gx", "gy")),
            P(("gx", "gy"), None),
            P(("gx", "gy")),
            P(("gx", "gy")),
            P(("gx", "gy")),
            P(None, ("gx", "gy")),
            P(("gx", "gy")),
        ),
        out_specs=(P(None, "gx", "gy"), P(("gx", "gy"), None)),
        check_vma=False,
    )
```

profile of v0, /device:TPU:1, one launch (start us, length us, event | category | flops | bytes accessed | tf_op | source)
XLA Modules:
  0.0 972.0 jit_solution(12247643676694862051)
XLA Ops:
  7.2 32.4 %all_gather.15 = s32[32768,1]{0,1:T(1,128)S(1)} all-gather(s32[1024,1]{0,1:T(1,128)} %param.14), channel_id=1, replica_groups=mesh['gx'=32,'gy'=16] {'gx'}, dimensions={0}, use_global_device_ids=true | all-gather | bytes 135168 | tf_op jit(solution)/shard_map/all_gather | solution.py:84
  40.3 1.3 dynamic-slice
  41.5 0.8 dynamic-update-slice
  42.3 13.0 %all-reduce = s32[32]{0:T(128)S(1)} all-reduce(s32[32]{0:T(128)S(1)} %dynamic-update-slice), channel_id=1, replica_groups=mesh['gx'=32,'gy'=16] {'gx'}, use_global_device_ids=true, to_apply=%add | all-reduce | flops 32 | bytes 256
  55.4 36.0 %all_gather.13 = f32[3,32768]{1,0:T(4,128)S(1)} all-gather(f32[3,1024]{1,0:T(4,128)} %param.13), channel_id=1, replica_groups=mesh['gx'=32,'gy'=16] {'gx'}, dimensions={1}, use_global_device_ids=true | all-gather | bytes 405504 | tf_op jit(solution)/shard_map/all_gather | solution.py:83
  91.4 0.4 compare_reduce_fusion
  91.8 0.1 multiply_bitcast_fusion
  92.0 8.6 copy.63
  100.6 29.8 %all_gather.12 = s32[32768]{0:T(1024)S(1)} all-gather(s32[1024]{0:T(1024)S(1)} %copy-done.6), channel_id=1, replica_groups=mesh['gx'=32,'gy'=16] {'gx'}, dimensions={0}, use_global_device_ids=true | all-gather | bytes 135168 | tf_op jit(solution)/shard_map/all_gather | solution.py:85
  130.4 176.4 %scatter_custom_fusion = f32[3,8192]{0,1:T(8,128)} fusion(s32[32768]{0:T(1024)S(1)} %compare_select_fusion, f32[32768,3]{1,0:T(8,128)} %copy.63, f32[]{:T(128)} %constant.12.clone.1), kind=kCustom, calls=%fused_computation.2 | custom fusion | flops 98304 | bytes 98816 | tf_op jit(solution)/shard_map/scatter-add | solution.py:91
  306.8 3.0 copy.66
  309.9 0.1 broadcast_multiply_fusion
  310.1 0.6 pad_maximum_fusion.21
  310.6 1.9 collective-permute-start
  312.6 0.6 pad_maximum_fusion.20
  313.2 1.3 collective-permute-start.1
  314.6 0.7 slice.525
  315.3 37.0 %collective-permute-start.2 = (f32[3,64,1]{2,1,0:T(8,128)}, f32[3,64,1]{2,1,0:T(8,128)S(1)}, u32[]{:S(2)}, u32[]{:S(2)}) collective-permute-start(f32[3,64,1]{2,1,0:T(8,128)} %slice.525), channel_id=1, source_target_pairs={{0,1},{1,2},{2,3},{3,4},{4,5},{5,6},{6,7},{7,8},{8,9},{9,10},{10,1... | collective-permute-start | bytes 2312 | tf_op jit(solution)/shard_map/ppermute | solution.py:12
  352.4 1.9 collective-permute-start.3
  354.3 0.7 multiply_add_fusion.32
  355.2 0.1 broadcast_multiply_fusion.1
  355.3 0.1 slice.536
  355.4 2.8 copy.65
  358.3 0.3 mul.732
  358.6 0.1 fusion.28
  358.7 0.1 fusion.27
  358.9 1.8 multiply_reduce_fusion.1
  360.7 104.9 %all-reduce.1 = (f32[]{:T(128)}, f32[]{:T(128)}) all-reduce(f32[]{:T(128)} %get-tuple-element.3, f32[]{:T(128)} %get-tuple-element.2), channel_id=1, replica_groups=mesh['gx'=32,'gy'=16] {'gx','gy'}, use_global_device_ids=true, to_apply=%region_2.3 | all-reduce | flops 2 | bytes 16 | tf_op jit(solution)/shard_map/psum | solution.py:62
  467.0 0.7 multiply_reduce_fusion
  467.7 95.7 %psum.37 = f32[]{:T(128)} all-reduce(f32[]{:T(128)} %get-tuple-element.6), channel_id=1, replica_groups=mesh['gx'=32,'gy'=16] {'gx','gy'}, use_global_device_ids=true, to_apply=%region_6.7 | all-reduce | flops 1 | bytes 8 | tf_op jit(solution)/shard_map/psum | solution.py:62
  564.7 0.9 fusion.21
  565.9 2.8 collective-permute-start.4
  568.7 1.3 collective-permute-start.5
  570.1 3.7 collective-permute-start.6
  573.9 1.9 collective-permute-start.7
  575.8 0.1 maximum_bitcast_fusion.1
  575.9 3.9 collective-permute-done.7
  579.8 0.1 maximum_bitcast_fusion.2
  580.0 0.9 fusion.7
  580.9 100.0 %psum.38 = f32[]{:T(128)} all-reduce(f32[]{:T(128)} %fusion.7), channel_id=1, replica_groups=mesh['gx'=32,'gy'=16] {'gx','gy'}, use_global_device_ids=true, to_apply=%region_8.9 | all-reduce | flops 1 | bytes 8 | tf_op jit(solution)/shard_map/psum | solution.py:101
  682.3 2.6 copy.69
  684.9 7.7 gather_fusion
  692.6 1.8 fusion.2
  694.4 0.1 reshape.251
  694.5 1.2 fusion.4
  695.7 0.7 multiply_add_fusion.2
  696.4 267.5 %all-reduce.4.cloned.1.call-done = f32[512,192]{1,0:T(8,128)} async-done(((f32[512,192]{1,0:T(8,128)}), f32[512,192]{1,0:T(8,128)}) %all-reduce.4.cloned.1.call-update) | async-done | bytes 393232 | tf_op jit(solution)/shard_map/psum | solution.py:123
  963.9 1.3 constant_dynamic-slice_fusion
  (64 shorter events, 1.1 us)
Async XLA Ops:
  7.2 956.7 %all-reduce.4.cloned.1.call-start = ((), (), s32[]{:S(2)}) async-start(), calls=%async_computation | async-start | bytes 1048576 | tf_op jit(solution)/shard_map/psum | solution.py:123
  92.0 8.6 copy-start.6
  306.8 3.0 copy-start
  306.8 3.0 copy-start.3
  306.8 3.0 copy-start.1
  310.6 48.2 %collective-permute-start = (f32[3,1,128]{2,1,0:T(1,128)}, f32[3,1,128]{2,1,0:T(1,128)S(1)}, u32[]{:S(2)}, u32[]{:S(2)}) collective-permute-start(f32[3,1,128]{2,1,0:T(1,128)} %pad_maximum_fusion.21), channel_id=1, source_target_pairs={{0,16},{16,32},{32,48},{48,64},{64,80},{80,96},{96,112},{112,128},... | collective-permute-start | bytes 4616 | tf_op jit(solution)/shard_map/ppermute | solution.py:12
  312.6 42.3 %copy-start.5 = (s32[2048]{0:T(1024)S(1)}, s32[2048]{0:T(1024)}, u32[]{:S(2)}) copy-start(s32[2048]{0:T(1024)} %param.17) | copy-start | bytes 24580
  312.6 42.3 %copy-start.4 = (f32[3,2048]{1,0:T(4,128)S(1)}, f32[3,2048]{1,0:T(4,128)}, u32[]{:S(2)}) copy-start(f32[3,2048]{1,0:T(4,128)} %param.18) | copy-start | bytes 73732
  313.2 45.6 %collective-permute-start.1 = (f32[3,1,128]{2,1,0:T(1,128)}, f32[3,1,128]{2,1,0:T(1,128)S(1)}, u32[]{:S(2)}, u32[]{:S(2)}) collective-permute-start(f32[3,1,128]{2,1,0:T(1,128)} %pad_maximum_fusion.20), channel_id=1, source_target_pairs={{16,0},{32,16},{48,32},{64,48},{80,64},{96,80},{112,96},{128,112},... | collective-permute-start | bytes 4616 | tf_op jit(solution)/shard_map/ppermute | solution.py:12
  315.3 43.3 %collective-permute-start.2 = (f32[3,64,1]{2,1,0:T(8,128)}, f32[3,64,1]{2,1,0:T(8,128)S(1)}, u32[]{:S(2)}, u32[]{:S(2)}) collective-permute-start(f32[3,64,1]{2,1,0:T(8,128)} %slice.525), channel_id=1, source_target_pairs={{0,1},{1,2},{2,3},{3,4},{4,5},{5,6},{6,7},{7,8},{8,9},{9,10},{10,1... | collective-permute-start | bytes 2312 | tf_op jit(solution)/shard_map/ppermute | solution.py:12
  352.4 6.4 collective-permute-start.3
  358.6 206.1 %copy-start.2 = (f32[1,64,128]{2,1,0:T(8,128)S(1)}, f32[1,64,128]{2,1,0:T(8,128)}, u32[]{:S(2)}) copy-start(f32[1,64,128]{2,1,0:T(8,128)} %get-tuple-element.37) | copy-start | bytes 98308
  565.9 14.1 %collective-permute-start.4 = (f32[3,1,128]{2,1,0:T(1,128)S(1)}, f32[3,1,128]{2,1,0:T(1,128)S(1)}, u32[]{:S(2)}, u32[]{:S(2)}) collective-permute-start(f32[3,1,128]{2,1,0:T(1,128)S(1)} %pad_maximum_fusion.19), channel_id=1, source_target_pairs={{0,16},{16,32},{32,48},{48,64},{64,80},{80,96},{96,112},{112,128},... | collective-permute-start | bytes 4616 | tf_op jit(solution)/shard_map/ppermute | solution.py:12
  568.7 11.3 %collective-permute-start.5 = (f32[3,1,128]{2,1,0:T(1,128)S(1)}, f32[3,1,128]{2,1,0:T(1,128)S(1)}, u32[]{:S(2)}, u32[]{:S(2)}) collective-permute-start(f32[3,1,128]{2,1,0:T(1,128)S(1)} %pad_maximum_fusion.18), channel_id=1, source_target_pairs={{16,0},{32,16},{48,32},{64,48},{80,64},{96,80},{112,96},{128,112},... | collective-permute-start | bytes 4616 | tf_op jit(solution)/shard_map/ppermute | solution.py:12
  570.1 5.7 collective-permute-start.6
  573.9 5.9 collective-permute-start.7
  684.9 9.6 copy-start.7
Sparse Core Ops, SparseCore 0:
  695.8 267.9 all-reduce.3
where the time goes:
time: 973 us; the launch traced here: 972 us
  blocking collectives  412 us (42%)
  waiting for transfers between devices  271 us (28%)
  other arithmetic  185 us (19%)
  starting transfers between devices  51.9 us (5%)
  local copies, waits for them, and re-layouts  29.5 us (3%)
  between operations  19.3 us (2%)
    psum x1, waiting for transfers between devices, per_device(): totals = lax.psum(partial_boxes, ('gx', 'gy'))  267 us
    psum x2, blocking collectives, residual_sum(): return lax.psum(jnp.sum(residual * precond), ('gx', 'gy'))  201 us
    scatter-add x1, other arithmetic, per_device(): flat_load.at[:, all_node].add(all_values * keeper.astype(jnp.float32))  176 us
    psum x1, blocking collectives, per_device(): step_size = norm_now / lax.psum(jnp.sum(search * image), ('gx', 'gy'))  100 us
    ppermute x8, starting transfers between devices, passed_along(): return lax.ppermute(block, axis, route)  51.8 us
    all_gather x1, blocking collectives, per_device(): lax.all_gather(src_values, 'gx', axis=1, tiled=True)  36 us
    all_gather x1, blocking collectives, per_device(): lax.all_gather(src_owner, 'gx', axis=0, tiled=True)  32.4 us
    all_gather x1, blocking collectives, per_device(): lax.all_gather(src_node, 'gx', axis=0, tiled=True)  29.8 us
  transfers between devices with their start and end apart: 9, of which 2 were waited for; matrix products, arithmetic and copies ran while one was open for 1% of the time, Pallas kernels for 0%

commit v1 on v0

v1 whole, which is shorter than its diff:
```python
import functools

import jax
import jax.numpy as jnp
from jax import lax
from jax.experimental import pallas as pl
from jax.experimental.pallas import tpu as pltpu
from jax.sharding import PartitionSpec as P

F32 = jnp.float32
BF16 = jnp.bfloat16
NT = (((1,), (1,)), ((), ()))


def halves(value):
    high = value.astype(BF16)
    low = (value - high.astype(F32)).astype(BF16)
    return high, low


def iota(shape, dim):
    return lax.broadcasted_iota(jnp.int32, shape, dim)


def mm(a, b, dims=(((1,), (0,)), ((), ()))):
    return lax.dot_general(a, b, dims, preferred_element_type=F32)


def kernel(
    sizes,
    count_ref,
    box_ref,
    diag_ref,
    edge_ref,
    mask_ref,
    val_ref,
    owner_ref,
    node_ref,
    surf_ref,
    param_ref,
    field_ref,
    grad_ref,
    v8_ref,
    bin_ref,
    ry_ref,
    pack_ref,
    rx_ref,
    halo_s,
    halo_r,
    sum_s,
    sum_y,
    sum_x,
    sum_z,
    sum_c,
    weight_ref,
    by_ref,
    bxs_ref,
    bxr_ref,
    bzs_ref,
    bzr_ref,
    bcs_ref,
    bcr_ref,
    send_sem,
    recv_sem,
):
    yn, xn, zn, cn = sizes
    gx, gy = lax.axis_index("gx"), lax.axis_index("gy")
    my, mx = gx // xn, gx % xn
    mz, mc = gy // cn, gy % cn

    def to_y(d):
        return (((my + d) % yn) * xn + mx, gy)

    def to_x(d):
        return (my * xn + (mx + d) % xn, gy)

    def to_z(d):
        return (gx, ((mz + d) % zn) * cn + mc)

    def to_c(d):
        return (gx, mz * cn + (mc + d) % cn)

    around = [
        ((gx + 1) % (yn * xn), gy),
        ((gx + yn * xn - 1) % (yn * xn), gy),
        (gx, (gy + 1) % (zn * cn)),
        (gx, (gy + zn * cn - 1) % (zn * cn)),
    ]
    axes = [(to_y, yn), (to_x, xn), (to_z, zn), (to_c, cn)]

    barrier = pltpu.get_barrier_semaphore()
    greeted = 0
    for target, size in axes:
        for d in range(1, size):
            pl.semaphore_signal(
                barrier, inc=1, device_id=target(d), device_id_type=pl.DeviceIdType.MESH
            )
            greeted += 1
    for target in around:
        pl.semaphore_signal(barrier, inc=1, device_id=target, device_id_type=pl.DeviceIdType.MESH)
        greeted += 1

    used = [0]

    def send(src, dst, target):
        slot = used[0]
        used[0] += 1
        copy = pltpu.make_async_remote_copy(
            src_ref=src,
            dst_ref=dst,
            send_sem=send_sem.at[slot],
            recv_sem=recv_sem.at[slot],
            device_id=target,
            device_id_type=pl.DeviceIdType.MESH,
        )
        copy.start()
        return copy

    def finish(copies):
        for copy in copies:
            copy.wait()

    owners = yn * xn
    v8_ref[...] = jnp.zeros_like(v8_ref)
    v8_ref[0:3, :] = val_ref[...]
    nodes = node_ref[...]
    v8_ref[3:4, :] = (nodes >> 7).astype(F32)
    v8_ref[4:5, :] = (nodes & 127).astype(F32)
    rows = nodes.shape[1]
    live = iota((1, rows), 1) < count_ref[0]
    owner = jnp.where(live, owner_ref[...], -1)
    upper = (iota((128, 128), 0) <= iota((128, 128), 1)).astype(BF16)
    before = jnp.zeros((owners, 1), F32)
    binned = jnp.zeros((owners * 8, 128), F32)
    for b in range(rows // 128):
        cut = slice(128 * b, 128 * b + 128)
        hot = (iota((owners, 128), 0) == owner[:, cut]).astype(F32)
        order = mm(hot.astype(BF16), upper) + before
        before = before + jnp.sum(hot, axis=1, keepdims=True)
        rank = jnp.sum(hot * order, axis=0, keepdims=True) - 1.0
        place = (iota((128, 128), 0).astype(F32) == rank).astype(BF16)
        part = v8_ref[:, cut]
        spread = (hot[:, None, :] * part[None, :, :]).reshape(owners * 8, 128)
        high, low = halves(spread)
        binned = binned + mm(high, place, NT) + mm(low, place, NT)
    bin_ref[...] = binned.reshape(yn, xn, 8, 128)

    pl.semaphore_wait(barrier, greeted)
    copies = [
        send(bin_ref.at[(my + d) % yn], ry_ref.at[d], to_y(d)) for d in range(1, yn)
    ]
    ry_ref[0] = bin_ref[my]

    def bern(coord, index):
        other = 1.0 - coord
        return jnp.where(
            index == 0,
            other * other * other,
            jnp.where(
                index == 1,
                3.0 * coord * other * other,
                jnp.where(index == 2, 3.0 * coord * coord * other, coord * coord * coord),
            ),
        )

    tiles = surf_ref.shape[0]
    line = iota((64, 128), 0)

    def weights(t, carry):
        cut = pl.ds(pl.multiple_of(t * 128, 128), 128)
        first = bern(param_ref[0:1, cut], line // 16)
        second = bern(param_ref[1:2, cut], (line // 4) % 4)
        third = bern(param_ref[2:3, cut], line % 4)
        weight_ref[t] = first * second * third
        return carry

    lax.fori_loop(0, tiles, weights, 0)

    finish(copies)
    for i in range(yn // 2):
        for e in range(xn):
            pack_ref[e, i] = ry_ref[2 * i, e] + pltpu.roll(ry_ref[2 * i + 1, e], 64, 1)
    copies = [
        send(pack_ref.at[(mx + d) % xn], rx_ref.at[d], to_x(d)) for d in range(1, xn)
    ]
    rx_ref[0] = pack_ref[mx]
    finish(copies)

    per = yn // 2

    def scatter(t, total):
        tile = rx_ref[t // per, t % per]
        row_hot = iota((64, 128), 0).astype(F32) == tile[3:4, :]
        col_hot = (iota((128, 128), 0).astype(F32) == tile[4:5, :]).astype(BF16)
        left = jnp.concatenate(
            [jnp.where(row_hot, tile[c : c + 1, :], 0.0) for c in range(3)], axis=0
        )
        high, low = halves(left)
        return total + mm(high, col_hot, NT) + mm(low, col_hot, NT)

    load = lax.fori_loop(0, xn * per, scatter, jnp.zeros((192, 128), F32))
    comps = range(3)
    residual = [load[64 * c : 64 * c + 64] for c in comps]

    row_id, lane_id = iota((64, 128), 0), iota((64, 128), 1)
    same = row_id == lane_id
    zero_rows = jnp.zeros((5, 128), F32)

    def operator(field, h):
        def product(d):
            keep = mask_ref[d].astype(F32)
            return [
                keep
                * (
                    edge_ref[d, c] * field[0]
                    + edge_ref[d, 3 + c] * field[1]
                    + edge_ref[d, 6 + c] * field[2]
                )
                for c in comps
            ]

        up_x, low_x, up_y, low_y = product(0), product(1), product(2), product(3)

        def column(value, lane):
            wide = jnp.broadcast_to(value[:, lane : lane + 1], (64, 128))
            return jnp.sum(jnp.where(same, wide, 0.0), axis=0, keepdims=True)

        outgoing = [
            [up_x[c][63:64, :] for c in comps],
            [low_x[c][0:1, :] for c in comps],
            [column(up_y[c], 127) for c in comps],
            [column(low_y[c], 0) for c in comps],
        ]
        copies = []
        for k in range(4):
            halo_s[h, k] = jnp.concatenate(outgoing[k] + [zero_rows], axis=0)
        for k in range(4):
            copies.append(send(halo_s.at[h, k], halo_r.at[h, k], around[k]))
        inner = [
            diag_ref[c] * field[0] + diag_ref[3 + c] * field[1] + diag_ref[6 + c] * field[2]
            for c in comps
        ]
        finish(copies)
        there = [gx > 0, gx < yn * xn - 1, gy > 0, gy < zn * cn - 1]
        got = [halo_r[h, k] * there[k].astype(F32) for k in range(4)]

        def upright(row):
            wide = jnp.broadcast_to(row, (64, 128))
            return jnp.sum(jnp.where(same, wide, 0.0), axis=1, keepdims=True)

        return [
            inner[c]
            + jnp.where(row_id == 0, got[0][c : c + 1, :], pltpu.roll(up_x[c], 1, 0))
            + jnp.where(row_id == 63, got[1][c : c + 1, :], pltpu.roll(low_x[c], 63, 0))
            + jnp.where(lane_id == 0, upright(got[2][c : c + 1, :]), pltpu.roll(up_y[c], 1, 1))
            + jnp.where(
                lane_id == 127, upright(got[3][c : c + 1, :]), pltpu.roll(low_y[c], 127, 1)
            )
            for c in comps
        ]

    def partial(pairs):
        total = None
        for a, b in pairs:
            for c in comps:
                total = a[c] * b[c] if total is None else total + a[c] * b[c]
        return jnp.sum(total, axis=0, keepdims=True)

    def total_sums(lines, h):
        pad = jnp.zeros((8 - len(lines), 128), F32)
        total = jnp.concatenate(lines + [pad], axis=0)
        for stage, landing in enumerate((sum_y, sum_x, sum_z, sum_c)):
            target, size = axes[stage]
            sum_s[h, stage] = total
            copies = [
                send(sum_s.at[h, stage], landing.at[h, d - 1], target(d)) for d in range(1, size)
            ]
            finish(copies)
            for d in range(1, size):
                total = total + landing[h, d - 1]
        total = jnp.sum(total, axis=1, keepdims=True)
        return [total[q : q + 1, :] for q in range(len(lines))]

    scale = [diag_ref[0], diag_ref[4], diag_ref[8]]
    search = [residual[c] / scale[c] for c in comps]
    image = operator(search, 0)
    norm, bend = total_sums([partial([(residual, search)]), partial([(search, image)])], 0)
    step = norm / bend
    residual = [residual[c] - step * image[c] for c in comps]
    precond = [residual[c] / scale[c] for c in comps]
    image_z = operator(precond, 1)
    norm_next, bend_z, bend_mix = total_sums(
        [
            partial([(residual, precond)]),
            partial([(precond, image_z)]),
            partial([(precond, image), (search, image_z)]),
        ],
        1,
    )
    turn = norm_next / norm
    step_next = norm_next / (bend_z + turn * bend_mix + turn * turn * bend)
    answer = [
        step * search[c] + step_next * (precond[c] + turn * search[c]) for c in comps
    ]
    for c in comps:
        field_ref[c] = answer[c]

    high, low = halves(jnp.concatenate(answer, axis=0))
    stacked = jnp.concatenate([high, low], axis=0)

    def term(t, total):
        node = surf_ref[pl.ds(t, 1), :]
        row_hot = iota((64, 128), 0) == (node >> 7)
        col_hot = (iota((128, 128), 0) == (node & 127)).astype(BF16)
        picked = mm(stacked, col_hot)
        weight = weight_ref[t]
        parts = []
        for c in comps:
            at = picked[64 * c : 64 * c + 64] + picked[192 + 64 * c : 256 + 64 * c]
            value = jnp.sum(jnp.where(row_hot, at, 0.0), axis=0, keepdims=True)
            parts.append(weight * value)
        parts.append(jnp.where(lane_id == 0, box_ref[t].astype(F32), 0.0))
        part_high, part_low = halves(jnp.concatenate(parts, axis=0))
        here = (iota((tiles, 128), 0) == t).astype(BF16)
        return total + mm(here, part_high, NT) + mm(here, part_low, NT)

    terms = lax.fori_loop(0, tiles, term, jnp.zeros((tiles, 256), F32))
    by_ref[0] = terms
    copies = [send(by_ref.at[0], by_ref.at[d], to_y(d)) for d in range(1, yn)]
    finish(copies)
    every = by_ref[...].reshape(yn * tiles, 256)
    per_y, per_x, per_z = xn * zn * cn, zn * cn, cn
    box = every[:, 192:193]
    wanted = (my * per_y + iota((yn * tiles, 128), 1)).astype(F32)
    chosen = jnp.transpose((box == wanted).astype(F32))[:per_y].astype(BF16)
    high, low = halves(every)
    dense = mm(chosen, high) + mm(chosen, low)
    bxs_ref[...] = dense.reshape(xn, per_x, 256)
    copies = [send(bxs_ref.at[(mx + d) % xn], bxr_ref.at[d - 1], to_x(d)) for d in range(1, xn)]
    dense = bxs_ref[mx]
    finish(copies)
    for d in range(1, xn):
        dense = dense + bxr_ref[d - 1]
    bzs_ref[...] = jnp.zeros_like(bzs_ref)
    for k in range(zn):
        bzs_ref[k, 0:per_z, :] = dense[k * per_z : (k + 1) * per_z, :]
    copies = [send(bzs_ref.at[(mz + d) % zn], bzr_ref.at[d - 1], to_z(d)) for d in range(1, zn)]
    dense = bzs_ref[mz]
    finish(copies)
    for d in range(1, zn):
        dense = dense + bzr_ref[d - 1]
    bcs_ref[...] = dense
    copies = [send(bcs_ref, bcr_ref, to_c(1))]
    finish(copies)
    dense = dense + bcr_ref[...]
    grad_ref[...] = jnp.where(mc == 0, dense[0:1, 0:192], dense[1:2, 0:192])


def per_device(
    sizes,
    diag_blocks,
    edge_blocks,
    edge_mask,
    src_values,
    src_owner,
    src_node,
    src_count,
    surf_node,
    surf_param,
    tile_box,
):
    yn, xn, zn, cn = sizes
    tiles = tile_box.shape[0]
    rows = src_node.shape[0]
    vmem = pl.BlockSpec(memory_space=pltpu.VMEM)
    smem = pl.BlockSpec(memory_space=pltpu.SMEM)
    copies = 2 * (yn + xn - 2 + 2) + (yn + xn + zn + cn - 4) * 3 + 8
    per_x = zn * cn

    def buf(*shape):
        return pltpu.VMEM(shape, F32)

    return pl.pallas_call(
        functools.partial(kernel, sizes),
        out_shape=(
            jax.ShapeDtypeStruct(diag_blocks.shape[:0] + (3,) + diag_blocks.shape[1:], F32),
            jax.ShapeDtypeStruct((1, 192), F32),
        ),
        in_specs=[smem, smem] + [vmem] * 8,
        out_specs=(vmem, vmem),
        scratch_shapes=[
            buf(8, rows),
            buf(yn, xn, 8, 128),
            buf(yn, xn, 8, 128),
            buf(xn, yn // 2, 8, 128),
            buf(xn, yn // 2, 8, 128),
            buf(2, 4, 8, 128),
            buf(2, 4, 8, 128),
            buf(2, 4, 8, 128),
            buf(2, yn - 1, 8, 128),
            buf(2, xn - 1, 8, 128),
            buf(2, zn - 1, 8, 128),
            buf(2, cn - 1, 8, 128),
            buf(tiles, 64, 128),
            buf(yn, tiles, 256),
            buf(xn, per_x, 256),
            buf(xn - 1, per_x, 256),
            buf(zn, 8, 256),
            buf(zn - 1, 8, 256),
            buf(8, 256),
            buf(8, 256),
            pltpu.SemaphoreType.DMA((copies,)),
            pltpu.SemaphoreType.DMA((copies,)),
        ],
        compiler_params=pltpu.CompilerParams(
            collective_id=0, has_side_effects=True, vmem_limit_bytes=32 * 2**20
        ),
    )(
        src_count,
        tile_box,
        diag_blocks,
        edge_blocks,
        edge_mask,
        src_values,
        src_owner.reshape(1, rows),
        src_node.reshape(1, rows),
        surf_node.reshape(tiles, 128),
        surf_param,
    )


def solution(mesh):
    across, along = mesh.shape["gx"], mesh.shape["gy"]
    xn = 4 if across >= 16 else 2
    sizes = (across // xn, xn, along // 2, 2)
    return jax.shard_map(
        functools.partial(per_device, sizes),
        mesh=mesh,
        in_specs=(
            P(None, "gx", "gy"),
            P(None, None, "gx", "gy"),
            P(None, "gx", "gy"),
            P(None, ("gx", "gy")),
            P(("gx", "gy"), None),
            P(("gx", "gy")),
            P(("gx", "gy")),
            P(("gx", "gy")),
            P(None, ("gx", "gy")),
            P(("gx", "gy")),
        ),
        out_specs=(P(None, "gx", "gy"), P(("gx", "gy"), None)),
        check_vma=False,
    )
```

time: 973 us -> 98.8 us (0.10)
  blocking collectives: 412 us -> 0 us
  waiting for transfers between devices: 271 us -> 0 us
  other arithmetic: 185 us -> 0 us
  Pallas kernels: 0 us -> 88.5 us
  starting transfers between devices: 51.9 us -> 0 us
  local copies, waits for them, and re-layouts: 29.5 us -> 8.53 us
  between operations: 19.3 us -> 1.3 us
    psum x3 -> x0, blocking collectives: 301 us -> none  [the longest x2 201 us: residual_sum(): return lax.psum(jnp.sum(residual * precond), ('gx', 'gy'))]
    psum x1 -> x0, waiting for transfers between devices: 267 us -> none  [per_device(): totals = lax.psum(partial_boxes, ('gx', 'gy'))]
    scatter-add x1 -> x0, other arithmetic: 176 us -> none  [per_device(): flat_load.at[:, all_node].add(all_values * keeper.astype(jnp.float32))]
    all_gather x3 -> x0, blocking collectives: 98.2 us -> none  [the longest x1 36 us: per_device(): lax.all_gather(src_values, 'gx', axis=1, tiled=True)]
    pallas_call x0 -> x1, Pallas kernels: none -> 88.5 us  [per_device(): pl.pallas_call(functools.partial(kernel, sizes), out_shape=(jax.ShapeDtyp...]
    ppermute x8 -> x0, starting transfers between devices: 51.8 us -> none  [passed_along(): return lax.ppermute(block, axis, route)]
    unnamed x1 -> x0, blocking collectives: 13 us -> none
  transfers between devices with their start and end apart: 9 -> 0, of which waited for: 2 -> 0; matrix products, arithmetic and copies ran while one was open for 1% -> 0% of each run, Pallas kernels for 0% -> 0%
where the time goes in v1:
time: 98.8 us; the launch traced here: 98.4 us
  Pallas kernels  88.5 us (90%)
  local copies, waits for them, and re-layouts  8.53 us (9%)
  between operations  1.3 us (1%)
    pallas_call x1, Pallas kernels, per_device(): pl.pallas_call(functools.partial(kernel, sizes), out_shape=(jax.ShapeDtyp...  88.5 us
    unnamed x20, local copies, waits for them, and re-layouts  8.53 us

profile of v1, /device:TPU:1, one launch (start us, length us, event | category | flops | bytes accessed | tf_op | source)
XLA Modules:
  0.0 98.4 jit_solution(15490474382300065074)
XLA Ops:
  1.3 0.0 copy-start
  1.3 1.3 %copy-done = f32[4,9,64,128]{3,2,1,0:T(8,128)S(1)} copy-done((f32[4,9,64,128]{3,2,1,0:T(8,128)S(1)}, f32[4,9,64,128]{3,2,1,0:T(8,128)}, u32[]{:S(2)}) %copy-start) | copy-done | bytes 1179672
  2.6 0.0 copy-start.1
  2.6 1.0 copy-done.1
  3.5 0.0 copy-start.2
  3.5 0.9 copy-done.2
  4.4 0.0 copy-start.3
  4.4 0.8 copy-done.3
  5.2 0.0 copy-start.4
  5.2 0.7 copy-done.4
  5.9 0.0 copy-start.5
  5.9 0.7 copy-done.5
  6.6 0.0 copy-start.6
  6.6 0.7 copy-done.6
  7.3 0.0 copy-start.7
  7.3 0.7 copy-done.7
  8.0 0.0 copy-start.8
  8.0 0.7 copy-done.8
  8.6 88.5 %shard_map.113 = (f32[3,64,128]{2,1,0:T(8,128)S(1)}, f32[1,192]{1,0:T(1,128)S(1)}) custom-call(s32[1]{0:T(128)S(6)} %copy.14.count_ref, s32[16]{0:T(128)S(1)} %copy-done.8, f32[9,64,128]{2,1,0:T(8,128)S(1)} %copy-done.1, f32[4,9,64,128]{3,2,1,0:T(8,128)S(1)} %copy-done, s32[4,64,128]{2,1,0:T(8,128)S(1)} %copy-done.2, f32[3,1024]{1,0:T(4,128)S(1)} %copy-done.4, ...), custom_call_target="tpu_custom_call" | custom-call | tf_op jit(solution)/shard_map/pallas_call | solution.py:383
  97.2 0.6 copy.15
  97.8 0.6 copy.16
Async XLA Ops:
  1.3 1.3 %copy-start = (f32[4,9,64,128]{3,2,1,0:T(8,128)S(1)}, f32[4,9,64,128]{3,2,1,0:T(8,128)}, u32[]{:S(2)}) copy-start(f32[4,9,64,128]{3,2,1,0:T(8,128)} %edge_ref.1) | copy-start | bytes 3538948
  2.6 1.0 copy-start.1
  3.5 0.9 copy-start.2
  4.4 0.8 copy-start.3
  5.2 0.7 copy-start.4
  5.9 0.7 copy-start.5
  6.6 0.7 copy-start.6
  7.3 0.7 copy-start.7
  8.0 0.7 copy-start.8

commit v2 on v1

v2 whole, which is shorter than its diff:
```python
import functools

import jax
import jax.numpy as jnp
from jax import lax
from jax.experimental import pallas as pl
from jax.experimental.pallas import tpu as pltpu
from jax.sharding import PartitionSpec as P

F32 = jnp.float32
BF16 = jnp.bfloat16
NT = (((1,), (1,)), ((), ()))


def halves(value):
    high = value.astype(BF16)
    low = (value - high.astype(F32)).astype(BF16)
    return high, low


def iota(shape, dim):
    return lax.broadcasted_iota(jnp.int32, shape, dim)


def mm(a, b, dims=(((1,), (0,)), ((), ()))):
    return lax.dot_general(a, b, dims, preferred_element_type=F32)


def kernel(
    sizes,
    count_hbm,
    box_hbm,
    diag_hbm,
    edge_hbm,
    mask_hbm,
    val_hbm,
    owner_hbm,
    node_hbm,
    surf_hbm,
    param_hbm,
    field_ref,
    grad_ref,
    count_ref,
    box_ref,
    diag_ref,
    edge_ref,
    mask_ref,
    val_ref,
    owner_ref,
    node_ref,
    surf_ref,
    param_ref,
    v8_ref,
    bin_ref,
    ry_ref,
    rx_ref,
    halo_s,
    halo_r,
    sum_s,
    sum_y,
    sum_x,
    sum_z,
    sum_c,
    weight_ref,
    by_ref,
    bxs_ref,
    bxr_ref,
    bzs_ref,
    bzr_ref,
    bcs_ref,
    bcr_ref,
    load_sem,
    send_sem,
    recv_sem,
):
    yn, xn, zn, cn = sizes
    gx, gy = lax.axis_index("gx"), lax.axis_index("gy")
    my, mx = gx // xn, gx % xn
    mz, mc = gy // cn, gy % cn

    def to_y(d):
        return (((my + d) % yn) * xn + mx, gy)

    def to_x(d):
        return (my * xn + (mx + d) % xn, gy)

    def to_z(d):
        return (gx, ((mz + d) % zn) * cn + mc)

    def to_c(d):
        return (gx, mz * cn + (mc + d) % cn)

    around = [
        ((gx + 1) % (yn * xn), gy),
        ((gx + yn * xn - 1) % (yn * xn), gy),
        (gx, (gy + 1) % (zn * cn)),
        (gx, (gy + zn * cn - 1) % (zn * cn)),
    ]
    axes = [(to_y, yn), (to_x, xn), (to_z, zn), (to_c, cn)]

    moved = [
        (count_hbm, count_ref),
        (owner_hbm, owner_ref),
        (node_hbm, node_ref),
        (val_hbm, val_ref),
        (param_hbm, param_ref),
        (mask_hbm, mask_ref),
        (edge_hbm, edge_ref),
        (diag_hbm, diag_ref),
        (surf_hbm, surf_ref),
        (box_hbm, box_ref),
    ]
    loads = [
        pltpu.make_async_copy(src, dst, load_sem.at[n]) for n, (src, dst) in enumerate(moved)
    ]
    for copy in loads:
        copy.start()

    barrier = pltpu.get_barrier_semaphore()
    greeted = 0
    for target, size in axes:
        for d in range(1, size):
            pl.semaphore_signal(
                barrier, inc=1, device_id=target(d), device_id_type=pl.DeviceIdType.MESH
            )
            greeted += 1
    for target in around:
        pl.semaphore_signal(barrier, inc=1, device_id=target, device_id_type=pl.DeviceIdType.MESH)
        greeted += 1

    used = [0]

    def send(src, dst, target):
        slot = used[0]
        used[0] += 1
        copy = pltpu.make_async_remote_copy(
            src_ref=src,
            dst_ref=dst,
            send_sem=send_sem.at[slot],
            recv_sem=recv_sem.at[slot],
            device_id=target,
            device_id_type=pl.DeviceIdType.MESH,
        )
        copy.start()
        return copy

    def finish(copies):
        for copy in copies:
            copy.wait()

    owners = yn * xn
    for copy in loads[:4]:
        copy.wait()
    v8_ref[...] = jnp.zeros_like(v8_ref)
    nodes = node_ref[...]
    v8_ref[0, 0:1, :] = val_ref[0:1, :]
    v8_ref[0, 1:2, :] = val_ref[2:3, :]
    v8_ref[1, 0:1, :] = val_ref[1:2, :]
    v8_ref[1, 1:2, :] = nodes.astype(F32)
    rows = nodes.shape[1]
    live = iota((1, rows), 1) < count_ref[...]
    owner = jnp.where(live, owner_ref[...], -1)
    upper = (iota((128, 128), 0) <= iota((128, 128), 1)).astype(BF16)
    before = jnp.zeros((owners, 1), F32)
    binned = jnp.zeros((owners * 8, 128), F32)
    for b in range(rows // 128):
        cut = slice(128 * b, 128 * b + 128)
        hot = (iota((owners, 128), 0) == owner[:, cut]).astype(F32)
        order = mm(hot.astype(BF16), upper) + before
        before = before + jnp.sum(hot, axis=1, keepdims=True)
        rank = jnp.sum(hot * order, axis=0, keepdims=True) - 1.0
        for half in range(2):
            spot = jnp.where(rank < 0.0, -1.0, rank + 64.0 * half)
            place = (iota((128, 128), 0).astype(F32) == spot).astype(BF16)
            part = v8_ref[half, :, cut]
            spread = (hot[:, None, :] * part[None, :, :]).reshape(owners * 8, 128)
            high, low = halves(spread)
            binned = binned + mm(high, place, NT) + mm(low, place, NT)
    bin_ref[...] = binned.reshape(yn, xn, 8, 128)[:, :, 0:2, :]

    pl.semaphore_wait(barrier, greeted)
    copies = [
        send(bin_ref.at[(my + d) % yn], ry_ref.at[d], to_y(d)) for d in range(1, yn)
    ]
    ry_ref[0] = bin_ref[my]

    def bern(coord, index):
        other = 1.0 - coord
        return jnp.where(
            index == 0,
            other * other * other,
            jnp.where(
                index == 1,
                3.0 * coord * other * other,
                jnp.where(index == 2, 3.0 * coord * coord * other, coord * coord * coord),
            ),
        )

    tiles = surf_ref.shape[0]
    line = iota((64, 128), 0)

    def weights(t, carry):
        cut = pl.ds(pl.multiple_of(t * 128, 128), 128)
        first = bern(param_ref[0:1, cut], line // 16)
        second = bern(param_ref[1:2, cut], (line // 4) % 4)
        third = bern(param_ref[2:3, cut], line % 4)
        weight_ref[t] = first * second * third
        return carry

    loads[4].wait()
    lax.fori_loop(0, tiles, weights, 0)

    for copy in loads[5:]:
        copy.wait()
    for d in range(4):
        keep = mask_ref[d].astype(F32)
        for n in range(9):
            edge_ref[d, n] = edge_ref[d, n] * keep

    finish(copies)
    copies = [
        send(ry_ref.at[:, (mx + d) % xn], rx_ref.at[d], to_x(d)) for d in range(1, xn)
    ]
    rx_ref[0] = ry_ref[:, mx]
    finish(copies)

    per = yn // 2
    left_half = iota((2, 128), 1) < 64

    def scatter(t, total):
        one, two = rx_ref[t // per, 2 * (t % per)], rx_ref[t // per, 2 * (t % per) + 1]
        near = jnp.where(left_half, one, pltpu.roll(two, 64, 1))
        far = jnp.where(left_half, pltpu.roll(one, 64, 1), two)
        node = far[1:2, :].astype(jnp.int32)
        row_hot = iota((64, 128), 0) == (node >> 7)
        col_hot = (iota((128, 128), 0) == (node & 127)).astype(BF16)
        values = [near[0:1, :], far[0:1, :], near[1:2, :]]
        left = jnp.concatenate([jnp.where(row_hot, v, 0.0) for v in values], axis=0)
        high, low = halves(left)
        return total + mm(high, col_hot, NT) + mm(low, col_hot, NT)

    load = lax.fori_loop(0, xn * per, scatter, jnp.zeros((192, 128), F32))
    comps = range(3)
    residual = [load[64 * c : 64 * c + 64] for c in comps]

    row_id, lane_id = iota((64, 128), 0), iota((64, 128), 1)
    same = row_id == lane_id
    zero_rows = jnp.zeros((5, 128), F32)

    def operator(field, h):
        def product(d):
            return [
                edge_ref[d, c] * field[0]
                + edge_ref[d, 3 + c] * field[1]
                + edge_ref[d, 6 + c] * field[2]
                for c in comps
            ]

        up_x, low_x, up_y, low_y = product(0), product(1), product(2), product(3)

        def column(value, lane):
            wide = jnp.broadcast_to(value[:, lane : lane + 1], (64, 128))
            return jnp.sum(jnp.where(same, wide, 0.0), axis=0, keepdims=True)

        outgoing = [
            [up_x[c][63:64, :] for c in comps],
            [low_x[c][0:1, :] for c in comps],
            [column(up_y[c], 127) for c in comps],
            [column(low_y[c], 0) for c in comps],
        ]
        copies = []
        for k in range(4):
            halo_s[h, k] = jnp.concatenate(outgoing[k] + [zero_rows], axis=0)
        for k in range(4):
            copies.append(send(halo_s.at[h, k], halo_r.at[h, k], around[k]))
        inner = [
            sum(diag_ref[3 * k + c] * field[k] for k in comps if k != c) for c in comps
        ]
        finish(copies)
        there = [gx > 0, gx < yn * xn - 1, gy > 0, gy < zn * cn - 1]
        got = [halo_r[h, k] * there[k].astype(F32) for k in range(4)]

        def upright(row):
            wide = jnp.broadcast_to(row, (64, 128))
            return jnp.sum(jnp.where(same, wide, 0.0), axis=1, keepdims=True)

        return [
            inner[c]
            + jnp.where(row_id == 0, got[0][c : c + 1, :], pltpu.roll(up_x[c], 1, 0))
            + jnp.where(row_id == 63, got[1][c : c + 1, :], pltpu.roll(low_x[c], 63, 0))
            + jnp.where(lane_id == 0, upright(got[2][c : c + 1, :]), pltpu.roll(up_y[c], 1, 1))
            + jnp.where(
                lane_id == 127, upright(got[3][c : c + 1, :]), pltpu.roll(low_y[c], 127, 1)
            )
            for c in comps
        ]

    def partial(a, b):
        return jnp.sum(a[0] * b[0] + a[1] * b[1] + a[2] * b[2], axis=0, keepdims=True)

    scale = [diag_ref[0], diag_ref[4], diag_ref[8]]
    search = [residual[c] / scale[c] for c in comps]
    other = operator(search, 0)
    second = [other[c] / scale[c] for c in comps]
    third = operator(second, 1)
    lines = [
        partial(search, residual),
        partial(search, other),
        partial(second, other),
        partial(search, third),
        partial(second, third),
    ]
    total = jnp.concatenate(lines + [jnp.zeros((8 - len(lines), 128), F32)], axis=0)
    for shift in (64, 32, 16):
        total = total + pltpu.roll(total, shift, 1)
    group = iota((8, 128), 1) // 16 == iota((8, 128), 0)
    total = jnp.sum(jnp.where(group, total, 0.0), axis=0, keepdims=True)

    pieces = halves(jnp.concatenate(search, axis=0)) + halves(jnp.concatenate(second, axis=0))
    stacked = jnp.concatenate(pieces, axis=0)

    def term(t, terms):
        node = surf_ref[pl.ds(t, 1), :]
        row_hot = iota((64, 128), 0) == (node >> 7)
        col_hot = (iota((128, 128), 0) == (node & 127)).astype(BF16)
        picked = mm(stacked, col_hot)
        weight = weight_ref[t]
        parts = []
        for first in (0, 384):
            for c in comps:
                at = first + 64 * c
                both = picked[at : at + 64] + picked[at + 192 : at + 256]
                value = jnp.sum(jnp.where(row_hot, both, 0.0), axis=0, keepdims=True)
                parts.append(weight * value)
        high, low = halves(jnp.concatenate(parts, axis=0))
        here = (iota((tiles, 128), 0) == t).astype(BF16)
        return terms + mm(here, high, NT) + mm(here, low, NT)

    terms = jnp.zeros((tiles, 384), F32)
    share = tiles // 4
    for stage, landing in enumerate((sum_y, sum_x, sum_z, sum_c)):
        target, size = axes[stage]
        sum_s[stage] = total
        copies = [send(sum_s.at[stage], landing.at[d - 1], target(d)) for d in range(1, size)]
        terms = lax.fori_loop(stage * share, (stage + 1) * share, term, terms)
        finish(copies)
        for d in range(1, size):
            total = total + landing[d - 1]
    total = jnp.where(group, jnp.broadcast_to(total, (8, 128)), 0.0)
    total = jnp.sum(total, axis=1, keepdims=True)
    norm, bend_a, bend_b, bend_c, bend_d = [total[q : q + 1, :] for q in range(5)]

    whole = norm + bend_a
    step = norm / whole
    rest = bend_a / whole
    norm_next = (norm / whole) * ((norm * bend_b - bend_a * bend_a) / whole)
    turn = norm_next / norm
    front = rest + turn
    bend_next = (
        front * front * whole
        - front * step * (2.0 * bend_a + bend_c + bend_b)
        + step * step * (bend_b + bend_d)
    )
    step_next = norm_next / bend_next
    alpha = step + step_next * front
    gamma = step * step_next

    match = iota((tiles, tiles), 0) == iota((tiles, tiles), 1)
    wide = jnp.broadcast_to(box_ref[...].astype(F32), (tiles, tiles))
    boxes = jnp.sum(jnp.where(match, wide, 0.0), axis=1, keepdims=True)
    terms = alpha * terms[:, 0:192] - gamma * terms[:, 192:384]
    terms = jnp.concatenate([terms, jnp.broadcast_to(boxes, (tiles, 64))], axis=1)
    by_ref[0] = terms
    copies = [send(by_ref.at[0], by_ref.at[d], to_y(d)) for d in range(1, yn)]
    for c in comps:
        field_ref[c] = alpha * search[c] - gamma * second[c]
    finish(copies)
    every = by_ref[...].reshape(yn * tiles, 256)
    per_y, per_x, per_z = xn * zn * cn, zn * cn, cn
    box = every[:, 192:193]
    wanted = (my * per_y + iota((yn * tiles, 128), 1)).astype(F32)
    chosen = jnp.transpose((box == wanted).astype(F32))[:per_y].astype(BF16)
    high, low = halves(every)
    dense = mm(chosen, high) + mm(chosen, low)
    bxs_ref[...] = dense.reshape(xn, per_x, 256)
    copies = [send(bxs_ref.at[(mx + d) % xn], bxr_ref.at[d - 1], to_x(d)) for d in range(1, xn)]
    dense = bxs_ref[mx]
    finish(copies)
    for d in range(1, xn):
        dense = dense + bxr_ref[d - 1]
    for k in range(zn):
        bzs_ref[k] = dense[k * per_z : (k + 1) * per_z, :]
    copies = [send(bzs_ref.at[(mz + d) % zn], bzr_ref.at[d - 1], to_z(d)) for d in range(1, zn)]
    dense = bzs_ref[mz]
    finish(copies)
    for d in range(1, zn):
        dense = dense + bzr_ref[d - 1]
    bcs_ref[...] = jnp.where(mc == 0, dense[1:2, :], dense[0:1, :])
    copies = [send(bcs_ref, bcr_ref, to_c(1))]
    dense = jnp.where(mc == 0, dense[0:1, :], dense[1:2, :])
    finish(copies)
    grad_ref[...] = (dense + bcr_ref[...])[:, 0:192]


def per_device(
    sizes,
    diag_blocks,
    edge_blocks,
    edge_mask,
    src_values,
    src_owner,
    src_node,
    src_count,
    surf_node,
    surf_param,
    tile_box,
):
    yn, xn, zn, cn = sizes
    tiles = tile_box.shape[0]
    rows = src_node.shape[0]
    vmem = pl.BlockSpec(memory_space=pltpu.VMEM)
    copies = 2 * (yn + xn - 2) + (yn + xn + zn + cn - 4) * 2 + 8
    per_x = zn * cn

    def buf(*shape):
        return pltpu.VMEM(shape, F32)

    operands = (
        src_count.reshape(1, 1),
        tile_box.reshape(1, tiles),
        diag_blocks,
        edge_blocks,
        edge_mask,
        src_values,
        src_owner.reshape(1, rows),
        src_node.reshape(1, rows),
        surf_node.reshape(tiles, 128),
        surf_param,
    )
    return pl.pallas_call(
        functools.partial(kernel, sizes),
        out_shape=(
            jax.ShapeDtypeStruct((3,) + diag_blocks.shape[1:], F32),
            jax.ShapeDtypeStruct((1, 192), F32),
        ),
        in_specs=[pl.BlockSpec(memory_space=pl.ANY)] * len(operands),
        out_specs=(vmem, vmem),
        scratch_shapes=[pltpu.VMEM(x.shape, x.dtype) for x in operands]
        + [
            buf(2, 8, rows),
            buf(yn, xn, 2, 128),
            buf(yn, xn, 2, 128),
            buf(xn, yn, 2, 128),
            buf(2, 4, 8, 128),
            buf(2, 4, 8, 128),
            buf(4, 1, 128),
            buf(yn - 1, 1, 128),
            buf(xn - 1, 1, 128),
            buf(zn - 1, 1, 128),
            buf(cn - 1, 1, 128),
            buf(tiles, 64, 128),
            buf(yn, tiles, 256),
            buf(xn, per_x, 256),
            buf(xn - 1, per_x, 256),
            buf(zn, cn, 256),
            buf(zn - 1, cn, 256),
            buf(1, 256),
            buf(1, 256),
            pltpu.SemaphoreType.DMA((len(operands),)),
            pltpu.SemaphoreType.DMA((copies,)),
            pltpu.SemaphoreType.DMA((copies,)),
        ],
        compiler_params=pltpu.CompilerParams(
            collective_id=0, has_side_effects=True, vmem_limit_bytes=60 * 2**20
        ),
    )(*operands)


def solution(mesh):
    across, along = mesh.shape["gx"], mesh.shape["gy"]
    xn = 4 if across >= 16 else 2
    sizes = (across // xn, xn, along // 2, 2)
    return jax.shard_map(
        functools.partial(per_device, sizes),
        mesh=mesh,
        in_specs=(
            P(None, "gx", "gy"),
            P(None, None, "gx", "gy"),
            P(None, "gx", "gy"),
            P(None, ("gx", "gy")),
            P(("gx", "gy"), None),
            P(("gx", "gy")),
            P(("gx", "gy")),
            P(("gx", "gy")),
            P(None, ("gx", "gy")),
            P(("gx", "gy")),
        ),
        out_specs=(P(None, "gx", "gy"), P(("gx", "gy"), None)),
        check_vma=False,
    )
```

time: 98.8 us -> 73.4 us (0.74)
  Pallas kernels: 88.5 us -> 69.2 us
  local copies, waits for them, and re-layouts: 8.53 us -> 2.78 us
    pallas_call x1, Pallas kernels: 88.5 us -> 69.2 us  [per_device(): pl.pallas_call(functools.partial(kernel, sizes), out_shape=(jax.ShapeDtyp...]
    unnamed x20 -> x2, local copies, waits for them, and re-layouts: 8.53 us -> 2.78 us
where the time goes in v2:
time: 73.4 us; the launch traced here: 73.2 us
  Pallas kernels  69.2 us (94%)
  local copies, waits for them, and re-layouts  2.78 us (4%)
  between operations  1.29 us (2%)
    pallas_call x1, Pallas kernels, per_device(): pl.pallas_call(functools.partial(kernel, sizes), out_shape=(jax.ShapeDtyp...  69.2 us
    unnamed x2, local copies, waits for them, and re-layouts  2.78 us

profile of v2, /device:TPU:1, one launch (start us, length us, event | category | flops | bytes accessed | tf_op | source)
XLA Modules:
  0.0 73.2 jit_solution(934035355923924338)
XLA Ops:
  1.3 69.2 %shard_map.113 = (f32[3,64,128]{2,1,0:T(8,128)}, f32[1,192]{1,0:T(1,128)}) custom-call(s32[1,1]{1,0:T(1,128)} %bitcast.5.count_hbm, s32[1,16]{1,0:T(1,128)} %bitcast.9, f32[9,64,128]{2,1,0:T(8,128)} %diag_hbm.1, f32[4,9,64,128]{3,2,1,0:T(8,128)} %edge_hbm.1, s32[4,64,128]{2,1,0:T(8,128)} %mask_hbm.1, f32[3,1024]{1,0:T(4,128)} %val_hbm.1, s32[1,1024]{1,0:T(1,128)} %bitcast.7, ...), custom_call_target="tpu_custom_call" | custom-call | tf_op jit(solution)/shard_map/pallas_call | solution.py:440
  70.4 1.5 %copy.15 = f32[3,64,128]{2,1,0:T(8,128)} copy(f32[3,64,128]{2,1,0:T(8,128)} %get-tuple-element.4) | data formatting | bytes 196608
  72.0 1.2 %copy.16 = f32[1,192]{1,0:T(1,128)} copy(f32[1,192]{1,0:T(1,128)} %get-tuple-element.5) | data formatting | bytes 1536

commit v3 on v2

--- a/solution.py
+++ b/solution.py
@@ -52,23 +52,18 @@
     param_ref,
     v8_ref,
     bin_ref,
-    ry_ref,
     rx_ref,
     halo_s,
     halo_r,
     sum_s,
+    sum_x,
     sum_y,
-    sum_x,
-    sum_z,
-    sum_c,
     weight_ref,
     by_ref,
     bxs_ref,
     bxr_ref,
     bzs_ref,
     bzr_ref,
-    bcs_ref,
-    bcr_ref,
     load_sem,
     send_sem,
     recv_sem,
@@ -76,7 +71,6 @@
     yn, xn, zn, cn = sizes
     gx, gy = lax.axis_index("gx"), lax.axis_index("gy")
     my, mx = gx // xn, gx % xn
-    mz, mc = gy // cn, gy % cn
 
     def to_y(d):
         return (((my + d) % yn) * xn + mx, gy)
@@ -84,11 +78,13 @@
     def to_x(d):
         return (my * xn + (mx + d) % xn, gy)
 
-    def to_z(d):
-        return (gx, ((mz + d) % zn) * cn + mc)
-
-    def to_c(d):
-        return (gx, mz * cn + (mc + d) % cn)
+    across, along = yn * xn, zn * cn
+
+    def to_gx(d):
+        return ((gx + d) % across, gy)
+
+    def to_gy(d):
+        return (gx, (gy + d) % along)
 
     around = [
         ((gx + 1) % (yn * xn), gy),
@@ -96,7 +92,7 @@
         (gx, (gy + 1) % (zn * cn)),
         (gx, (gy + zn * cn - 1) % (zn * cn)),
     ]
-    axes = [(to_y, yn), (to_x, xn), (to_z, zn), (to_c, cn)]
+    axes = [(to_gx, across), (to_gy, along)]
 
     moved = [
         (count_hbm, count_ref),
@@ -124,9 +120,6 @@
                 barrier, inc=1, device_id=target(d), device_id_type=pl.DeviceIdType.MESH
             )
             greeted += 1
-    for target in around:
-        pl.semaphore_signal(barrier, inc=1, device_id=target, device_id_type=pl.DeviceIdType.MESH)
-        greeted += 1
 
     used = [0]
 
@@ -148,7 +141,7 @@
         for copy in copies:
             copy.wait()
 
-    owners = yn * xn
+    owners = across
     for copy in loads[:4]:
         copy.wait()
     v8_ref[...] = jnp.zeros_like(v8_ref)
@@ -176,13 +169,13 @@
             spread = (hot[:, None, :] * part[None, :, :]).reshape(owners * 8, 128)
             high, low = halves(spread)
             binned = binned + mm(high, place, NT) + mm(low, place, NT)
-    bin_ref[...] = binned.reshape(yn, xn, 8, 128)[:, :, 0:2, :]
+    bin_ref[...] = binned.reshape(owners, 8, 128)[:, 0:2, :]
 
     pl.semaphore_wait(barrier, greeted)
     copies = [
-        send(bin_ref.at[(my + d) % yn], ry_ref.at[d], to_y(d)) for d in range(1, yn)
-    ]
-    ry_ref[0] = bin_ref[my]
+        send(bin_ref.at[(gx + d) % across], rx_ref.at[d], to_gx(d)) for d in range(1, across)
+    ]
+    rx_ref[0] = bin_ref[gx]
 
     def bern(coord, index):
         other = 1.0 - coord
@@ -218,17 +211,10 @@
             edge_ref[d, n] = edge_ref[d, n] * keep
 
     finish(copies)
-    copies = [
-        send(ry_ref.at[:, (mx + d) % xn], rx_ref.at[d], to_x(d)) for d in range(1, xn)
-    ]
-    rx_ref[0] = ry_ref[:, mx]
-    finish(copies)
-
-    per = yn // 2
     left_half = iota((2, 128), 1) < 64
 
     def scatter(t, total):
-        one, two = rx_ref[t // per, 2 * (t % per)], rx_ref[t // per, 2 * (t % per) + 1]
+        one, two = rx_ref[2 * t], rx_ref[2 * t + 1]
         near = jnp.where(left_half, one, pltpu.roll(two, 64, 1))
         far = jnp.where(left_half, pltpu.roll(one, 64, 1), two)
         node = far[1:2, :].astype(jnp.int32)
@@ -239,7 +225,7 @@
         high, low = halves(left)
         return total + mm(high, col_hot, NT) + mm(low, col_hot, NT)
 
-    load = lax.fori_loop(0, xn * per, scatter, jnp.zeros((192, 128), F32))
+    load = lax.fori_loop(0, owners // 2, scatter, jnp.zeros((192, 128), F32))
     comps = range(3)
     residual = [load[64 * c : 64 * c + 64] for c in comps]
 
@@ -248,33 +234,37 @@
     zero_rows = jnp.zeros((5, 128), F32)
 
     def operator(field, h):
-        def product(d):
+        def product(d, part=slice(0, 64)):
             return [
-                edge_ref[d, c] * field[0]
-                + edge_ref[d, 3 + c] * field[1]
-                + edge_ref[d, 6 + c] * field[2]
+                edge_ref[d, c, part] * field[0][part]
+                + edge_ref[d, 3 + c, part] * field[1][part]
+                + edge_ref[d, 6 + c, part] * field[2][part]
                 for c in comps
             ]
-
-        up_x, low_x, up_y, low_y = product(0), product(1), product(2), product(3)
 
         def column(value, lane):
             wide = jnp.broadcast_to(value[:, lane : lane + 1], (64, 128))
             return jnp.sum(jnp.where(same, wide, 0.0), axis=0, keepdims=True)
 
-        outgoing = [
-            [up_x[c][63:64, :] for c in comps],
-            [low_x[c][0:1, :] for c in comps],
-            [column(up_y[c], 127) for c in comps],
-            [column(low_y[c], 0) for c in comps],
+        def give(k, lines):
+            halo_s[h, k] = jnp.concatenate(lines + [zero_rows], axis=0)
+            return send(halo_s.at[h, k], halo_r.at[h, k], around[k])
+
+        copies = [
+            give(0, [line[7:8, :] for line in product(0, slice(56, 64))]),
+            give(1, [line[0:1, :] for line in product(1, slice(0, 8))]),
         ]
-        copies = []
-        for k in range(4):
-            halo_s[h, k] = jnp.concatenate(outgoing[k] + [zero_rows], axis=0)
-        for k in range(4):
-            copies.append(send(halo_s.at[h, k], halo_r.at[h, k], around[k]))
+        up_y, low_y = product(2), product(3)
+        copies.append(give(2, [column(up_y[c], 127) for c in comps]))
+        copies.append(give(3, [column(low_y[c], 0) for c in comps]))
+        up_x, low_x = product(0), product(1)
         inner = [
-            sum(diag_ref[3 * k + c] * field[k] for k in comps if k != c) for c in comps
+            sum(diag_ref[3 * k + c] * field[k] for k in comps if k != c)
+            + jnp.where(row_id == 0, 0.0, pltpu.roll(up_x[c], 1, 0))
+            + jnp.where(row_id == 63, 0.0, pltpu.roll(low_x[c], 63, 0))
+            + jnp.where(lane_id == 0, 0.0, pltpu.roll(up_y[c], 1, 1))
+            + jnp.where(lane_id == 127, 0.0, pltpu.roll(low_y[c], 127, 1))
+            for c in comps
         ]
         finish(copies)
         there = [gx > 0, gx < yn * xn - 1, gy > 0, gy < zn * cn - 1]
@@ -286,12 +276,10 @@
 
         return [
             inner[c]
-            + jnp.where(row_id == 0, got[0][c : c + 1, :], pltpu.roll(up_x[c], 1, 0))
-            + jnp.where(row_id == 63, got[1][c : c + 1, :], pltpu.roll(low_x[c], 63, 0))
-            + jnp.where(lane_id == 0, upright(got[2][c : c + 1, :]), pltpu.roll(up_y[c], 1, 1))
-            + jnp.where(
-                lane_id == 127, upright(got[3][c : c + 1, :]), pltpu.roll(low_y[c], 127, 1)
-            )
+            + jnp.where(row_id == 0, got[0][c : c + 1, :], 0.0)
+            + jnp.where(row_id == 63, got[1][c : c + 1, :], 0.0)
+            + jnp.where(lane_id == 0, upright(got[2][c : c + 1, :]), 0.0)
+            + jnp.where(lane_id == 127, upright(got[3][c : c + 1, :]), 0.0)
             for c in comps
         ]
 
@@ -337,12 +325,12 @@
         return terms + mm(here, high, NT) + mm(here, low, NT)
 
     terms = jnp.zeros((tiles, 384), F32)
-    share = tiles // 4
-    for stage, landing in enumerate((sum_y, sum_x, sum_z, sum_c)):
+    ends = [0, 9 * tiles // 16, tiles]
+    for stage, landing in enumerate((sum_x, sum_y)):
         target, size = axes[stage]
         sum_s[stage] = total
         copies = [send(sum_s.at[stage], landing.at[d - 1], target(d)) for d in range(1, size)]
-        terms = lax.fori_loop(stage * share, (stage + 1) * share, term, terms)
+        terms = lax.fori_loop(ends[stage], ends[stage + 1], term, terms)
         finish(copies)
         for d in range(1, size):
             total = total + landing[d - 1]
@@ -376,7 +364,7 @@
         field_ref[c] = alpha * search[c] - gamma * second[c]
     finish(copies)
     every = by_ref[...].reshape(yn * tiles, 256)
-    per_y, per_x, per_z = xn * zn * cn, zn * cn, cn
+    per_y, per_x = xn * along, along
     box = every[:, 192:193]
     wanted = (my * per_y + iota((yn * tiles, 128), 1)).astype(F32)
     chosen = jnp.transpose((box == wanted).astype(F32))[:per_y].astype(BF16)
@@ -388,18 +376,16 @@
     finish(copies)
     for d in range(1, xn):
         dense = dense + bxr_ref[d - 1]
-    for k in range(zn):
-        bzs_ref[k] = dense[k * per_z : (k + 1) * per_z, :]
-    copies = [send(bzs_ref.at[(mz + d) % zn], bzr_ref.at[d - 1], to_z(d)) for d in range(1, zn)]
-    dense = bzs_ref[mz]
+    for k in range(along):
+        bzs_ref[k] = dense[k : k + 1, :]
+    copies = [
+        send(bzs_ref.at[(gy + d) % along], bzr_ref.at[d - 1], to_gy(d)) for d in range(1, along)
+    ]
+    dense = bzs_ref[gy]
     finish(copies)
-    for d in range(1, zn):
+    for d in range(1, along):
         dense = dense + bzr_ref[d - 1]
-    bcs_ref[...] = jnp.where(mc == 0, dense[1:2, :], dense[0:1, :])
-    copies = [send(bcs_ref, bcr_ref, to_c(1))]
-    dense = jnp.where(mc == 0, dense[0:1, :], dense[1:2, :])
-    finish(copies)
-    grad_ref[...] = (dense + bcr_ref[...])[:, 0:192]
+    grad_ref[...] = dense[:, 0:192]
 
 
 def per_device(
@@ -419,8 +405,8 @@
     tiles = tile_box.shape[0]
     rows = src_node.shape[0]
     vmem = pl.BlockSpec(memory_space=pltpu.VMEM)
-    copies = 2 * (yn + xn - 2) + (yn + xn + zn + cn - 4) * 2 + 8
-    per_x = zn * cn
+    across, per_x = yn * xn, zn * cn
+    copies = 2 * (across - 1) + 2 * (per_x - 1) + yn + xn - 2 + 8
 
     def buf(*shape):
         return pltpu.VMEM(shape, F32)
@@ -448,24 +434,19 @@
         scratch_shapes=[pltpu.VMEM(x.shape, x.dtype) for x in operands]
         + [
             buf(2, 8, rows),
-            buf(yn, xn, 2, 128),
-            buf(yn, xn, 2, 128),
-            buf(xn, yn, 2, 128),
+            buf(across, 2, 128),
+            buf(across, 2, 128),
             buf(2, 4, 8, 128),
             buf(2, 4, 8, 128),
-            buf(4, 1, 128),
-            buf(yn - 1, 1, 128),
-            buf(xn - 1, 1, 128),
-            buf(zn - 1, 1, 128),
-            buf(cn - 1, 1, 128),
+            buf(2, 1, 128),
+            buf(across - 1, 1, 128),
+            buf(per_x - 1, 1, 128),
             buf(tiles, 64, 128),
             buf(yn, tiles, 256),
             buf(xn, per_x, 256),
             buf(xn - 1, per_x, 256),
-            buf(zn, cn, 256),
-            buf(zn - 1, cn, 256),
-            buf(1, 256),
-            buf(1, 256),
+            buf(per_x, 1, 256),
+            buf(per_x - 1, 1, 256),
             pltpu.SemaphoreType.DMA((len(operands),)),
             pltpu.SemaphoreType.DMA((copies,)),
             pltpu.SemaphoreType.DMA((copies,)),

time: 73.4 us -> 67.2 us (0.916)
  Pallas kernels: 69.2 us -> 62.9 us
    pallas_call x1, Pallas kernels: 69.2 us -> 62.9 us  [per_device(): pl.pallas_call(functools.partial(kernel, sizes), out_shape=(jax.ShapeDtyp...]
where the time goes in v3:
time: 67.2 us; the launch traced here: 67 us
  Pallas kernels  62.9 us (94%)
  local copies, waits for them, and re-layouts  2.78 us (4%)
  between operations  1.29 us (2%)
    pallas_call x1, Pallas kernels, per_device(): pl.pallas_call(functools.partial(kernel, sizes), out_shape=(jax.ShapeDtyp...  62.9 us
    unnamed x2, local copies, waits for them, and re-layouts  2.78 us

profile of v3, /device:TPU:1, one launch (start us, length us, event | category | flops | bytes accessed | tf_op | source)
XLA Modules:
  0.0 67.0 jit_solution(11858613512348513483)
XLA Ops:
  1.3 62.9 %shard_map.113 = (f32[3,64,128]{2,1,0:T(8,128)}, f32[1,192]{1,0:T(1,128)}) custom-call(s32[1,1]{1,0:T(1,128)} %bitcast.5.count_hbm, s32[1,16]{1,0:T(1,128)} %bitcast.9, f32[9,64,128]{2,1,0:T(8,128)} %diag_hbm.1, f32[4,9,64,128]{3,2,1,0:T(8,128)} %edge_hbm.1, s32[4,64,128]{2,1,0:T(8,128)} %mask_hbm.1, f32[3,1024]{1,0:T(4,128)} %val_hbm.1, s32[1,1024]{1,0:T(1,128)} %bitcast.7, ...), custom_call_target="tpu_custom_call" | custom-call | tf_op jit(solution)/shard_map/pallas_call | solution.py:426
  64.2 1.5 %copy.15 = f32[3,64,128]{2,1,0:T(8,128)} copy(f32[3,64,128]{2,1,0:T(8,128)} %get-tuple-element.4) | data formatting | bytes 196608
  65.8 1.2 %copy.16 = f32[1,192]{1,0:T(1,128)} copy(f32[1,192]{1,0:T(1,128)} %get-tuple-element.5) | data formatting | bytes 1536

commit v4 on v3

--- a/solution.py
+++ b/solution.py
@@ -59,6 +59,7 @@
     sum_x,
     sum_y,
     weight_ref,
+    id_ref,
     by_ref,
     bxs_ref,
     bxr_ref,
@@ -144,12 +145,13 @@
     owners = across
     for copy in loads[:4]:
         copy.wait()
-    v8_ref[...] = jnp.zeros_like(v8_ref)
     nodes = node_ref[...]
-    v8_ref[0, 0:1, :] = val_ref[0:1, :]
-    v8_ref[0, 1:2, :] = val_ref[2:3, :]
-    v8_ref[1, 0:1, :] = val_ref[1:2, :]
-    v8_ref[1, 1:2, :] = nodes.astype(F32)
+    lines = [val_ref[0:1, :], val_ref[2:3, :], val_ref[1:2, :], nodes.astype(F32)]
+    for n, line in enumerate(lines):
+        high, low = halves(line)
+        at = n % 2 + 4 * (n // 2)
+        v8_ref[at : at + 1, :] = high.astype(F32)
+        v8_ref[at + 2 : at + 3, :] = low.astype(F32)
     rows = nodes.shape[1]
     live = iota((1, rows), 1) < count_ref[...]
     owner = jnp.where(live, owner_ref[...], -1)
@@ -162,20 +164,26 @@
         order = mm(hot.astype(BF16), upper) + before
         before = before + jnp.sum(hot, axis=1, keepdims=True)
         rank = jnp.sum(hot * order, axis=0, keepdims=True) - 1.0
-        for half in range(2):
-            spot = jnp.where(rank < 0.0, -1.0, rank + 64.0 * half)
-            place = (iota((128, 128), 0).astype(F32) == spot).astype(BF16)
-            part = v8_ref[half, :, cut]
-            spread = (hot[:, None, :] * part[None, :, :]).reshape(owners * 8, 128)
-            high, low = halves(spread)
-            binned = binned + mm(high, place, NT) + mm(low, place, NT)
-    bin_ref[...] = binned.reshape(owners, 8, 128)[:, 0:2, :]
+        place = ((iota((128, 128), 0) & 63).astype(F32) == rank).astype(BF16)
+        spread = (hot[:, None, :] * v8_ref[:, cut][None, :, :]).reshape(owners * 8, 128)
+        binned = binned + mm(spread.astype(BF16), place, NT)
+    binned = binned.reshape(owners, 8, 128)
+    near = binned[:, 0:2, :] + binned[:, 2:4, :]
+    far = binned[:, 4:6, :] + binned[:, 6:8, :]
+    bin_ref[...] = jnp.where(iota((owners, 2, 128), 2) < 64, near, far)
 
     pl.semaphore_wait(barrier, greeted)
     copies = [
         send(bin_ref.at[(gx + d) % across], rx_ref.at[d], to_gx(d)) for d in range(1, across)
     ]
     rx_ref[0] = bin_ref[gx]
+
+    loads[9].wait()
+    tiles = surf_ref.shape[0]
+    ids = box_ref[...].astype(F32)
+    ids = jnp.concatenate([ids, jnp.zeros((1, 128 - tiles), F32)], axis=1)
+    id_ref[0] = ids
+    id_copies = [send(id_ref.at[0], id_ref.at[d], to_y(d)) for d in range(1, yn)]
 
     def bern(coord, index):
         other = 1.0 - coord
@@ -189,7 +197,6 @@
             ),
         )
 
-    tiles = surf_ref.shape[0]
     line = iota((64, 128), 0)
 
     def weights(t, carry):
@@ -203,7 +210,7 @@
     loads[4].wait()
     lax.fori_loop(0, tiles, weights, 0)
 
-    for copy in loads[5:]:
+    for copy in loads[5:9]:
         copy.wait()
     for d in range(4):
         keep = mask_ref[d].astype(F32)
@@ -211,21 +218,45 @@
             edge_ref[d, n] = edge_ref[d, n] * keep
 
     finish(copies)
+    finish(id_copies)
+    per_y, per_x = xn * along, along
+    lane = iota((1, 128), 1)
+    half = tiles // 2
+    id_all, id_low, id_high = ids, jnp.where(lane < half, ids, 0.0), None
+    id_high = pltpu.roll(jnp.where(lane < half, 0.0, ids), 128 - half, 1)
+    for d in range(1, yn):
+        ids = id_ref[d]
+        id_all = id_all + pltpu.roll(ids, tiles * d, 1)
+        id_low = id_low + pltpu.roll(jnp.where(lane < half, ids, 0.0), half * d, 1)
+        turned = jnp.where(lane < half, 0.0, ids)
+        id_high = id_high + pltpu.roll(turned, (128 + half * (d - 1)) % 128, 1)
+
+    def chosen(ids, width):
+        wanted = (my * per_y + iota((per_y, 128), 0)).astype(F32)
+        return (wanted == ids).astype(F32)[:, :width].astype(BF16)
+
+    pick_all = chosen(id_all, yn * tiles)
+    pick_low = chosen(id_low, yn * half)
+    pick_high = chosen(id_high, yn * half)
+
     left_half = iota((2, 128), 1) < 64
 
     def scatter(t, total):
-        one, two = rx_ref[2 * t], rx_ref[2 * t + 1]
-        near = jnp.where(left_half, one, pltpu.roll(two, 64, 1))
-        far = jnp.where(left_half, pltpu.roll(one, 64, 1), two)
-        node = far[1:2, :].astype(jnp.int32)
-        row_hot = iota((64, 128), 0) == (node >> 7)
-        col_hot = (iota((128, 128), 0) == (node & 127)).astype(BF16)
-        values = [near[0:1, :], far[0:1, :], near[1:2, :]]
-        left = jnp.concatenate([jnp.where(row_hot, v, 0.0) for v in values], axis=0)
-        high, low = halves(left)
-        return total + mm(high, col_hot, NT) + mm(low, col_hot, NT)
-
-    load = lax.fori_loop(0, owners // 2, scatter, jnp.zeros((192, 128), F32))
+        lefts, cols = [], []
+        for k in range(2):
+            one, two = rx_ref[4 * t + 2 * k], rx_ref[4 * t + 2 * k + 1]
+            near = jnp.where(left_half, one, pltpu.roll(two, 64, 1))
+            far = jnp.where(left_half, pltpu.roll(one, 64, 1), two)
+            node = far[1:2, :].astype(jnp.int32)
+            row_hot = iota((64, 128), 0) == (node >> 7)
+            cols.append((iota((128, 128), 0) == (node & 127)).astype(BF16))
+            values = [near[0:1, :], far[0:1, :], near[1:2, :]]
+            left = jnp.concatenate([jnp.where(row_hot, v, 0.0) for v in values], axis=0)
+            lefts.append(jnp.concatenate(halves(left), axis=0))
+        return total + mm(jnp.concatenate(lefts, axis=1), jnp.concatenate(cols, axis=1), NT)
+
+    load = lax.fori_loop(0, owners // 4, scatter, jnp.zeros((384, 128), F32))
+    load = load[0:192] + load[192:384]
     comps = range(3)
     residual = [load[64 * c : 64 * c + 64] for c in comps]
 
@@ -308,24 +339,31 @@
     stacked = jnp.concatenate(pieces, axis=0)
 
     def term(t, terms):
-        node = surf_ref[pl.ds(t, 1), :]
-        row_hot = iota((64, 128), 0) == (node >> 7)
-        col_hot = (iota((128, 128), 0) == (node & 127)).astype(BF16)
-        picked = mm(stacked, col_hot)
-        weight = weight_ref[t]
-        parts = []
-        for first in (0, 384):
-            for c in comps:
-                at = first + 64 * c
-                both = picked[at : at + 64] + picked[at + 192 : at + 256]
-                value = jnp.sum(jnp.where(row_hot, both, 0.0), axis=0, keepdims=True)
-                parts.append(weight * value)
-        high, low = halves(jnp.concatenate(parts, axis=0))
-        here = (iota((tiles, 128), 0) == t).astype(BF16)
+        nodes = [surf_ref[pl.ds(2 * t + k, 1), :] for k in range(2)]
+        cols = [(iota((128, 128), 0) == (node & 127)).astype(BF16) for node in nodes]
+        picked = mm(stacked, jnp.concatenate(cols, axis=1))
+        tops, bottoms, heres = [], [], []
+        for k in range(2):
+            row_hot = iota((64, 128), 0) == (nodes[k] >> 7)
+            weight = weight_ref[2 * t + k]
+            parts = []
+            for first in (0, 384):
+                for c in comps:
+                    at = first + 64 * c
+                    side = picked[:, 128 * k : 128 * k + 128]
+                    both = side[at : at + 64] + side[at + 192 : at + 256]
+                    value = jnp.sum(jnp.where(row_hot, both, 0.0), axis=0, keepdims=True)
+                    parts.append(weight * value)
+            high, low = halves(jnp.concatenate(parts, axis=0))
+            tops.append(high)
+            bottoms.append(low)
+            heres.append((iota((tiles, 128), 0) == 2 * t + k).astype(BF16))
+        here = jnp.concatenate(heres, axis=1)
+        high, low = jnp.concatenate(tops, axis=1), jnp.concatenate(bottoms, axis=1)
         return terms + mm(here, high, NT) + mm(here, low, NT)
 
     terms = jnp.zeros((tiles, 384), F32)
-    ends = [0, 9 * tiles // 16, tiles]
+    ends = [0, 5 * tiles // 16, tiles // 2]
     for stage, landing in enumerate((sum_x, sum_y)):
         target, size = axes[stage]
         sum_s[stage] = total
@@ -353,23 +391,20 @@
     alpha = step + step_next * front
     gamma = step * step_next
 
-    match = iota((tiles, tiles), 0) == iota((tiles, tiles), 1)
-    wide = jnp.broadcast_to(box_ref[...].astype(F32), (tiles, tiles))
-    boxes = jnp.sum(jnp.where(match, wide, 0.0), axis=1, keepdims=True)
     terms = alpha * terms[:, 0:192] - gamma * terms[:, 192:384]
-    terms = jnp.concatenate([terms, jnp.broadcast_to(boxes, (tiles, 64))], axis=1)
-    by_ref[0] = terms
+    by_ref[0, 0:tiles, :] = terms[:, 0:128]
+    by_ref[0, tiles:, :] = jnp.concatenate([terms[:half, 128:192], terms[half:, 128:192]], axis=1)
     copies = [send(by_ref.at[0], by_ref.at[d], to_y(d)) for d in range(1, yn)]
     for c in comps:
         field_ref[c] = alpha * search[c] - gamma * second[c]
     finish(copies)
-    every = by_ref[...].reshape(yn * tiles, 256)
-    per_y, per_x = xn * along, along
-    box = every[:, 192:193]
-    wanted = (my * per_y + iota((yn * tiles, 128), 1)).astype(F32)
-    chosen = jnp.transpose((box == wanted).astype(F32))[:per_y].astype(BF16)
-    high, low = halves(every)
-    dense = mm(chosen, high) + mm(chosen, low)
+    high, low = halves(by_ref[:, 0:tiles, :].reshape(yn * tiles, 128))
+    dense = mm(pick_all, high) + mm(pick_all, low)
+    high, low = halves(by_ref[:, tiles:, :].reshape(yn * half, 128))
+    near = mm(pick_low, high) + mm(pick_low, low)
+    far = mm(pick_high, high) + mm(pick_high, low)
+    near = jnp.where(iota(near.shape, 1) < 64, near + pltpu.roll(far, 64, 1), 0.0)
+    dense = jnp.concatenate([dense, near], axis=1)
     bxs_ref[...] = dense.reshape(xn, per_x, 256)
     copies = [send(bxs_ref.at[(mx + d) % xn], bxr_ref.at[d - 1], to_x(d)) for d in range(1, xn)]
     dense = bxs_ref[mx]
@@ -406,7 +441,7 @@
     rows = src_node.shape[0]
     vmem = pl.BlockSpec(memory_space=pltpu.VMEM)
     across, per_x = yn * xn, zn * cn
-    copies = 2 * (across - 1) + 2 * (per_x - 1) + yn + xn - 2 + 8
+    copies = 2 * (across - 1) + 2 * (per_x - 1) + 2 * (yn - 1) + xn - 1 + 8
 
     def buf(*shape):
         return pltpu.VMEM(shape, F32)
@@ -433,7 +468,7 @@
         out_specs=(vmem, vmem),
         scratch_shapes=[pltpu.VMEM(x.shape, x.dtype) for x in operands]
         + [
-            buf(2, 8, rows),
+            buf(8, rows),
             buf(across, 2, 128),
             buf(across, 2, 128),
             buf(2, 4, 8, 128),
@@ -442,7 +477,8 @@
             buf(across - 1, 1, 128),
             buf(per_x - 1, 1, 128),
             buf(tiles, 64, 128),
-            buf(yn, tiles, 256),
+            buf(yn, 1, 128),
+            buf(yn, tiles * 3 // 2, 128),
             buf(xn, per_x, 256),
             buf(xn - 1, per_x, 256),
             buf(per_x, 1, 256),

time: 67.2 us -> 65.1 us (0.969)
  Pallas kernels: 62.9 us -> 60.8 us
    pallas_call x1, Pallas kernels: 62.9 us -> 60.8 us  [per_device(): pl.pallas_call(functools.partial(kernel, sizes), out_shape=(jax.ShapeDtyp...]
where the time goes in v4:
time: 65.1 us; the launch traced here: 64.9 us
  Pallas kernels  60.8 us (93%)
  local copies, waits for them, and re-layouts  2.78 us (4%)
  between operations  1.29 us (2%)
    pallas_call x1, Pallas kernels, per_device(): pl.pallas_call(functools.partial(kernel, sizes), out_shape=(jax.ShapeDtyp...  60.8 us
    unnamed x2, local copies, waits for them, and re-layouts  2.78 us

profile of v4, /device:TPU:1, one launch (start us, length us, event | category | flops | bytes accessed | tf_op | source)
XLA Modules:
  0.0 64.9 jit_solution(15371479033841424975)
XLA Ops:
  1.3 60.8 %shard_map.113 = (f32[3,64,128]{2,1,0:T(8,128)}, f32[1,192]{1,0:T(1,128)}) custom-call(s32[1,1]{1,0:T(1,128)} %bitcast.5.count_hbm, s32[1,16]{1,0:T(1,128)} %bitcast.9, f32[9,64,128]{2,1,0:T(8,128)} %diag_hbm.1, f32[4,9,64,128]{3,2,1,0:T(8,128)} %edge_hbm.1, s32[4,64,128]{2,1,0:T(8,128)} %mask_hbm.1, f32[3,1024]{1,0:T(4,128)} %val_hbm.1, s32[1,1024]{1,0:T(1,128)} %bitcast.7, ...), custom_call_target="tpu_custom_call" | custom-call | tf_op jit(solution)/shard_map/pallas_call | solution.py:461
  62.1 1.5 %copy.15 = f32[3,64,128]{2,1,0:T(8,128)} copy(f32[3,64,128]{2,1,0:T(8,128)} %get-tuple-element.4) | data formatting | bytes 196608
  63.6 1.2 %copy.16 = f32[1,192]{1,0:T(1,128)} copy(f32[1,192]{1,0:T(1,128)} %get-tuple-element.5) | data formatting | bytes 1536

commit v5 on v4

--- a/solution.py
+++ b/solution.py
@@ -20,6 +20,10 @@
 
 def iota(shape, dim):
     return lax.broadcasted_iota(jnp.int32, shape, dim)
+
+
+def far_first(size):
+    return sorted(range(1, size), key=lambda d: abs(2 * d - size))
 
 
 def mm(a, b, dims=(((1,), (0,)), ((), ()))):
@@ -59,6 +63,7 @@
     sum_x,
     sum_y,
     weight_ref,
+    inv_ref,
     id_ref,
     by_ref,
     bxs_ref,
@@ -174,7 +179,7 @@
 
     pl.semaphore_wait(barrier, greeted)
     copies = [
-        send(bin_ref.at[(gx + d) % across], rx_ref.at[d], to_gx(d)) for d in range(1, across)
+        send(bin_ref.at[(gx + d) % across], rx_ref.at[d], to_gx(d)) for d in far_first(across)
     ]
     rx_ref[0] = bin_ref[gx]
 
@@ -183,7 +188,7 @@
     ids = box_ref[...].astype(F32)
     ids = jnp.concatenate([ids, jnp.zeros((1, 128 - tiles), F32)], axis=1)
     id_ref[0] = ids
-    id_copies = [send(id_ref.at[0], id_ref.at[d], to_y(d)) for d in range(1, yn)]
+    id_copies = [send(id_ref.at[0], id_ref.at[d], to_y(d)) for d in far_first(yn)]
 
     def bern(coord, index):
         other = 1.0 - coord
@@ -212,33 +217,14 @@
 
     for copy in loads[5:9]:
         copy.wait()
+    for n in range(3):
+        inv_ref[n] = 1.0 / diag_ref[4 * n]
     for d in range(4):
         keep = mask_ref[d].astype(F32)
         for n in range(9):
             edge_ref[d, n] = edge_ref[d, n] * keep
 
     finish(copies)
-    finish(id_copies)
-    per_y, per_x = xn * along, along
-    lane = iota((1, 128), 1)
-    half = tiles // 2
-    id_all, id_low, id_high = ids, jnp.where(lane < half, ids, 0.0), None
-    id_high = pltpu.roll(jnp.where(lane < half, 0.0, ids), 128 - half, 1)
-    for d in range(1, yn):
-        ids = id_ref[d]
-        id_all = id_all + pltpu.roll(ids, tiles * d, 1)
-        id_low = id_low + pltpu.roll(jnp.where(lane < half, ids, 0.0), half * d, 1)
-        turned = jnp.where(lane < half, 0.0, ids)
-        id_high = id_high + pltpu.roll(turned, (128 + half * (d - 1)) % 128, 1)
-
-    def chosen(ids, width):
-        wanted = (my * per_y + iota((per_y, 128), 0)).astype(F32)
-        return (wanted == ids).astype(F32)[:, :width].astype(BF16)
-
-    pick_all = chosen(id_all, yn * tiles)
-    pick_low = chosen(id_low, yn * half)
-    pick_high = chosen(id_high, yn * half)
-
     left_half = iota((2, 128), 1) < 64
 
     def scatter(t, total):
@@ -317,10 +303,9 @@
     def partial(a, b):
         return jnp.sum(a[0] * b[0] + a[1] * b[1] + a[2] * b[2], axis=0, keepdims=True)
 
-    scale = [diag_ref[0], diag_ref[4], diag_ref[8]]
-    search = [residual[c] / scale[c] for c in comps]
+    search = [residual[c] * inv_ref[c] for c in comps]
     other = operator(search, 0)
-    second = [other[c] / scale[c] for c in comps]
+    second = [other[c] * inv_ref[c] for c in comps]
     third = operator(second, 1)
     lines = [
         partial(search, residual),
@@ -362,12 +347,40 @@
         high, low = jnp.concatenate(tops, axis=1), jnp.concatenate(bottoms, axis=1)
         return terms + mm(here, high, NT) + mm(here, low, NT)
 
+    half = tiles // 2
+    per_y, per_x = xn * along, along
+
+    def box_picks():
+        finish(id_copies)
+        own = id_ref[0]
+        lane = iota((1, 128), 1)
+        id_all, id_low = own, jnp.where(lane < half, own, 0.0)
+        id_high = pltpu.roll(jnp.where(lane < half, 0.0, own), 128 - half, 1)
+        for d in range(1, yn):
+            line = id_ref[d]
+            id_all = id_all + pltpu.roll(line, tiles * d, 1)
+            id_low = id_low + pltpu.roll(jnp.where(lane < half, line, 0.0), half * d, 1)
+            turned = jnp.where(lane < half, 0.0, line)
+            id_high = id_high + pltpu.roll(turned, (128 + half * (d - 1)) % 128, 1)
+
+        def chosen(ids, width):
+            wanted = (my * per_y + iota((per_y, 128), 0)).astype(F32)
+            return (wanted == ids).astype(F32)[:, :width].astype(BF16)
+
+        return (
+            chosen(id_all, yn * tiles),
+            chosen(id_low, yn * half),
+            chosen(id_high, yn * half),
+        )
+
     terms = jnp.zeros((tiles, 384), F32)
     ends = [0, 5 * tiles // 16, tiles // 2]
     for stage, landing in enumerate((sum_x, sum_y)):
         target, size = axes[stage]
         sum_s[stage] = total
-        copies = [send(sum_s.at[stage], landing.at[d - 1], target(d)) for d in range(1, size)]
+        copies = [send(sum_s.at[stage], landing.at[d - 1], target(d)) for d in far_first(size)]
+        if stage == 1:
+            pick_all, pick_low, pick_high = box_picks()
         terms = lax.fori_loop(ends[stage], ends[stage + 1], term, terms)
         finish(copies)
         for d in range(1, size):
@@ -394,7 +407,7 @@
     terms = alpha * terms[:, 0:192] - gamma * terms[:, 192:384]
     by_ref[0, 0:tiles, :] = terms[:, 0:128]
     by_ref[0, tiles:, :] = jnp.concatenate([terms[:half, 128:192], terms[half:, 128:192]], axis=1)
-    copies = [send(by_ref.at[0], by_ref.at[d], to_y(d)) for d in range(1, yn)]
+    copies = [send(by_ref.at[0], by_ref.at[d], to_y(d)) for d in far_first(yn)]
     for c in comps:
         field_ref[c] = alpha * search[c] - gamma * second[c]
     finish(copies)
@@ -406,7 +419,7 @@
     near = jnp.where(iota(near.shape, 1) < 64, near + pltpu.roll(far, 64, 1), 0.0)
     dense = jnp.concatenate([dense, near], axis=1)
     bxs_ref[...] = dense.reshape(xn, per_x, 256)
-    copies = [send(bxs_ref.at[(mx + d) % xn], bxr_ref.at[d - 1], to_x(d)) for d in range(1, xn)]
+    copies = [send(bxs_ref.at[(mx + d) % xn], bxr_ref.at[d - 1], to_x(d)) for d in far_first(xn)]
     dense = bxs_ref[mx]
     finish(copies)
     for d in range(1, xn):
@@ -414,7 +427,7 @@
     for k in range(along):
         bzs_ref[k] = dense[k : k + 1, :]
     copies = [
-        send(bzs_ref.at[(gy + d) % along], bzr_ref.at[d - 1], to_gy(d)) for d in range(1, along)
+        send(bzs_ref.at[(gy + d) % along], bzr_ref.at[d - 1], to_gy(d)) for d in far_first(along)
     ]
     dense = bzs_ref[gy]
     finish(copies)
@@ -477,6 +490,7 @@
             buf(across - 1, 1, 128),
             buf(per_x - 1, 1, 128),
             buf(tiles, 64, 128),
+            buf(3, 64, 128),
             buf(yn, 1, 128),
             buf(yn, tiles * 3 // 2, 128),
             buf(xn, per_x, 256),

time: 65.1 us -> 63.9 us (0.982)
  Pallas kernels: 60.8 us -> 59.6 us
    pallas_call x1, Pallas kernels: 60.8 us -> 59.6 us  [per_device(): pl.pallas_call(functools.partial(kernel, sizes), out_shape=(jax.ShapeDtyp...]
where the time goes in v5:
time: 63.9 us; the launch traced here: 63.7 us
  Pallas kernels  59.6 us (93%)
  local copies, waits for them, and re-layouts  2.78 us (4%)
  between operations  1.29 us (2%)
    pallas_call x1, Pallas kernels, per_device(): pl.pallas_call(functools.partial(kernel, sizes), out_shape=(jax.ShapeDtyp...  59.6 us
    unnamed x2, local copies, waits for them, and re-layouts  2.78 us

profile of v5, /device:TPU:1, one launch (start us, length us, event | category | flops | bytes accessed | tf_op | source)
XLA Modules:
  0.0 63.7 jit_solution(13863306342486184133)
XLA Ops:
  1.3 59.6 %shard_map.113 = (f32[3,64,128]{2,1,0:T(8,128)}, f32[1,192]{1,0:T(1,128)}) custom-call(s32[1,1]{1,0:T(1,128)} %bitcast.5.count_hbm, s32[1,16]{1,0:T(1,128)} %bitcast.9, f32[9,64,128]{2,1,0:T(8,128)} %diag_hbm.1, f32[4,9,64,128]{3,2,1,0:T(8,128)} %edge_hbm.1, s32[4,64,128]{2,1,0:T(8,128)} %mask_hbm.1, f32[3,1024]{1,0:T(4,128)} %val_hbm.1, s32[1,1024]{1,0:T(1,128)} %bitcast.7, ...), custom_call_target="tpu_custom_call" | custom-call | tf_op jit(solution)/shard_map/pallas_call | solution.py:474
  60.9 1.5 %copy.15 = f32[3,64,128]{2,1,0:T(8,128)} copy(f32[3,64,128]{2,1,0:T(8,128)} %get-tuple-element.4) | data formatting | bytes 196608
  62.4 1.2 %copy.16 = f32[1,192]{1,0:T(1,128)} copy(f32[1,192]{1,0:T(1,128)} %get-tuple-element.5) | data formatting | bytes 1536

commit v6 on v5

--- a/solution.py
+++ b/solution.py
@@ -229,8 +229,8 @@
 
     def scatter(t, total):
         lefts, cols = [], []
-        for k in range(2):
-            one, two = rx_ref[4 * t + 2 * k], rx_ref[4 * t + 2 * k + 1]
+        for k in range(4):
+            one, two = rx_ref[8 * t + 2 * k], rx_ref[8 * t + 2 * k + 1]
             near = jnp.where(left_half, one, pltpu.roll(two, 64, 1))
             far = jnp.where(left_half, pltpu.roll(one, 64, 1), two)
             node = far[1:2, :].astype(jnp.int32)
@@ -241,7 +241,7 @@
             lefts.append(jnp.concatenate(halves(left), axis=0))
         return total + mm(jnp.concatenate(lefts, axis=1), jnp.concatenate(cols, axis=1), NT)
 
-    load = lax.fori_loop(0, owners // 4, scatter, jnp.zeros((384, 128), F32))
+    load = lax.fori_loop(0, owners // 8, scatter, jnp.zeros((384, 128), F32))
     load = load[0:192] + load[192:384]
     comps = range(3)
     residual = [load[64 * c : 64 * c + 64] for c in comps]

time: 63.9 us -> 62.9 us (0.984)
  Pallas kernels: 59.6 us -> 58.7 us
    pallas_call x1, Pallas kernels: 59.6 us -> 58.7 us  [per_device(): pl.pallas_call(functools.partial(kernel, sizes), out_shape=(jax.ShapeDtyp...]
where the time goes in v6:
time: 62.9 us; the launch traced here: 62.7 us
  Pallas kernels  58.7 us (93%)
  local copies, waits for them, and re-layouts  2.78 us (4%)
  between operations  1.29 us (2%)
    pallas_call x1, Pallas kernels, per_device(): pl.pallas_call(functools.partial(kernel, sizes), out_shape=(jax.ShapeDtyp...  58.7 us
    unnamed x2, local copies, waits for them, and re-layouts  2.78 us

profile of v6, /device:TPU:1, one launch (start us, length us, event | category | flops | bytes accessed | tf_op | source)
XLA Modules:
  0.0 62.7 jit_solution(14300428849714397000)
XLA Ops:
  1.3 58.7 %shard_map.113 = (f32[3,64,128]{2,1,0:T(8,128)}, f32[1,192]{1,0:T(1,128)}) custom-call(s32[1,1]{1,0:T(1,128)} %bitcast.5.count_hbm, s32[1,16]{1,0:T(1,128)} %bitcast.9, f32[9,64,128]{2,1,0:T(8,128)} %diag_hbm.1, f32[4,9,64,128]{3,2,1,0:T(8,128)} %edge_hbm.1, s32[4,64,128]{2,1,0:T(8,128)} %mask_hbm.1, f32[3,1024]{1,0:T(4,128)} %val_hbm.1, s32[1,1024]{1,0:T(1,128)} %bitcast.7, ...), custom_call_target="tpu_custom_call" | custom-call | tf_op jit(solution)/shard_map/pallas_call | solution.py:474
  60.0 1.5 %copy.15 = f32[3,64,128]{2,1,0:T(8,128)} copy(f32[3,64,128]{2,1,0:T(8,128)} %get-tuple-element.4) | data formatting | bytes 196608
  61.5 1.2 %copy.16 = f32[1,192]{1,0:T(1,128)} copy(f32[1,192]{1,0:T(1,128)} %get-tuple-element.5) | data formatting | bytes 1536
